TPU v7x, 32 devices: a whole 2x2x4 slice. The times are simulated.
32 devices in a mesh: context: 16 (over z, y, core), tensor: 2 (over x).
Axes of the slice: x: 2, y: 2, z: 4, core: 2. Of those that a mesh axis runs over, the one named last changes fastest.
Arguments:
- queries: bfloat16 [4096, 2048], P(('context', 'tensor')), may hold values from -6 to 6
- key_rows: bfloat16 [4096, 2048], P(('context', 'tensor')), may hold values from -6 to 6
- value_rows: bfloat16 [4096, 2048], P(('context', 'tensor')), may hold values from -6 to 6
- grad_output: bfloat16 [4096, 2048], P(('context', 'tensor')), may hold values from -6 to 6
Outputs:
- attended: bfloat16 [4096, 2048], P(('context', 'tensor'))
- grad_queries: bfloat16 [4096, 2048], P(('context', 'tensor'))
- grad_keys: bfloat16 [4096, 2048], P(('context', 'tensor'))
- grad_values: bfloat16 [4096, 2048], P(('context', 'tensor'))
All inputs are finite; a program needn't handle non-finite values.
Results may differ from a plain program's by a relative error of at most 0.007.
Values may be sent and summed in bfloat16 or wider, within the bound.
No kernel may reach another device: no remote copies, remote signals or barrier semaphores. Data moves between devices by JAX's collectives and lax.ppermute only.
A program may use at most 64 MiB of HBM per device.

v0:
```python
import functools

import jax
import jax.numpy as jnp
from jax import lax
from jax.experimental import pallas as pl
from jax.experimental.pallas import tpu as pltpu
from jax.sharding import PartitionSpec as P


DH = 128
AXES = ("context", "tensor")
PLANE = 8
GROUP = 4
OWNERS = 4

eps = 1e-06

F32 = jnp.float32
BF16 = jnp.bfloat16


def dot(a, b, contract):
    return lax.dot_general(a, b, ((contract[:1], contract[1:]), ((), ())), preferred_element_type=F32)


def pair_bit():
    pair = lax.axis_size(AXES[1]) if lax.axis_size(AXES[1]) < GROUP else 1
    return pair, (GROUP - 1) ^ pair, GROUP


def here():
    return lax.axis_index(AXES[0]) * lax.axis_size(AXES[1]) + lax.axis_index(AXES[1])


def has(bit):
    return jnp.bitwise_and(here(), bit) > 0


def owner_xor(r):
    _, near, far = pair_bit()
    return (near if r & 1 else 0) ^ (far if r & 2 else 0)


def owner():
    _, near, far = pair_bit()
    return has(near).astype(jnp.int32) + 2 * has(far).astype(jnp.int32)


def swap(x, bits):
    count = lax.axis_size(AXES[0]) * lax.axis_size(AXES[1])
    return lax.ppermute(x, AXES, [(i, i ^ bits) for i in range(count)])


def call(kernel, inputs, outs, flops=0, hbm_in=False, hbm_out=False, scratch=(), grant=16):
    space_in = pl.BlockSpec(memory_space=pl.ANY if hbm_in else pltpu.VMEM)
    space_out = pl.BlockSpec(memory_space=pl.ANY if hbm_out else pltpu.VMEM)
    moved = sum(a.size * a.dtype.itemsize for a in list(inputs) + list(outs))
    return pl.pallas_call(
        kernel,
        out_shape=list(outs),
        in_specs=[space_in] * len(inputs),
        out_specs=[space_out] * len(outs),
        scratch_shapes=list(scratch),
        compiler_params=pltpu.CompilerParams(vmem_limit_bytes=grant * 1024 * 1024),
        cost_estimate=pl.CostEstimate(flops=flops, bytes_accessed=moved, transcendentals=0),
    )(*inputs)


def share_columns(r, j, share):
    head = jnp.bitwise_xor(owner(), r) * share + j
    return head, pl.ds(pl.multiple_of(head * DH, DH), DH)


def causal_mask(rows):
    return lax.broadcasted_iota(jnp.int32, (rows, rows), 0) >= lax.broadcasted_iota(jnp.int32, (rows, rows), 1)


def run_copies(copies):
    for copy in copies:
        copy.start()
    for copy in copies:
        copy.wait()


def split_kernel(a, b, own, other, sems):
    half = own.shape[2]
    mine = has(pair_bit()[0]).astype(jnp.int32)
    copies = []
    for k, target in enumerate((other, own)):
        for n, source in enumerate((a, b)):
            at = pl.ds(pl.multiple_of((mine if k else 1 - mine) * half, half), half)
            copies.append(pltpu.make_async_copy(source.at[:, at], target.at[n], sems.at[n, k]))
    run_copies(copies)


def join_first_kernel(*refs):
    att_own, (dq_own, received), outs, sems = refs[:OWNERS], refs[OWNERS : OWNERS + 2], refs[OWNERS + 2 : -1], refs[-1]
    half, width = dq_own.shape[1], att_own[0].shape[1]
    mine = has(pair_bit()[0]).astype(jnp.int32)
    at = pl.ds(pl.multiple_of((1 - mine) * half, half), half)
    copies = [pltpu.make_async_copy(received.at[n], outs[n].at[:, at], sems.at[n]) for n in range(2)]
    at = pl.ds(pl.multiple_of(mine * half, half), half)
    copies.append(pltpu.make_async_copy(dq_own, outs[1].at[:, at], sems.at[2]))
    for r in range(OWNERS):
        at = pl.ds(pl.multiple_of(mine * half + jnp.bitwise_xor(owner(), r) * width, width), width)
        copies.append(pltpu.make_async_copy(att_own[r], outs[0].at[:, at], sems.at[3 + r]))
    run_copies(copies)


def join_last_kernel(*refs):
    own, received, outs, sems = refs[:OWNERS], refs[OWNERS : 2 * OWNERS], refs[2 * OWNERS : -1], refs[-1]
    width = own[0].shape[2]
    half = OWNERS * width
    mine = has(pair_bit()[0]).astype(jnp.int32)
    copies = []
    for r in range(OWNERS):
        for k, sources in enumerate((received, own)):
            start = (mine if k else 1 - mine) * half + jnp.bitwise_xor(owner(), r) * width
            for n in range(2):
                at = pl.ds(pl.multiple_of(start, width), width)
                copies.append(pltpu.make_async_copy(sources[r].at[n], outs[n].at[:, at], sems.at[r, k, n]))
    run_copies(copies)


def states_kernel(share, own, other, *outs):
    sums, every = outs[:OWNERS], outs[OWNERS]
    for r in range(OWNERS):
        for j in range(share):
            _, at = share_columns(r, j, share)
            first = dot(own[0, :, at], own[1, :, at], (0, 0))
            second = dot(other[0, :, at], other[1, :, at], (0, 0))
            every[r, 0, j] = first.astype(BF16)
            every[r, 1, j] = second.astype(BF16)
            sums[r][j] = (first + second).astype(BF16)


def sum_kernel(*refs):
    for j in range(refs[0].shape[0]):
        refs[-1][j] = sum(ref[j].astype(F32) for ref in refs[:-1]).astype(BF16)


def pack_kernel(*refs):
    for r in range(OWNERS):
        refs[-1][r] = refs[r][...]


def base_kernel(reverse, steps, *refs):
    count = len(steps)
    parts, others, (mine, across) = refs[:OWNERS], refs[OWNERS : OWNERS + count], refs[OWNERS + count :]
    late = has(pair_bit()[2])
    counts_far = jnp.logical_not(late) if reverse else late
    plane = here() // PLANE
    for j in range(mine.shape[0]):
        base = jnp.zeros(mine.shape[1:], F32)
        for other, step in zip(others, steps):
            source = jnp.bitwise_xor(plane, step)
            keep = source > plane if reverse else source < plane
            base = base + jnp.where(keep, other[j].astype(F32), 0.0)
        same = parts[0][j].astype(F32) + parts[1][j].astype(F32)
        far = parts[2][j].astype(F32) + parts[3][j].astype(F32)
        mine[j] = (base + jnp.where(counts_far, far, 0.0)).astype(BF16)
        across[j] = (base + jnp.where(counts_far, 0.0, same)).astype(BF16)


def local_kernel(reverse, every, direct, out):
    pair, near, _ = pair_bit()
    place = jnp.bitwise_and(here(), GROUP - 1)
    for r in range(OWNERS):
        for j in range(every.shape[2]):
            sources = [(0, every[r, 0, j]), (pair, every[r, 1, j])]
            sources += [(near, direct[r ^ 1, 0, j]), (near ^ pair, direct[r ^ 1, 1, j])]
            sources = [(mask, state.astype(F32)) for mask, state in sources]
            for n, target in enumerate((0, pair)):
                to = jnp.bitwise_xor(place, target)
                total = jnp.zeros(every.shape[3:], F32)
                for mask, state in sources:
                    if mask != target:
                        source = jnp.bitwise_xor(place, mask)
                        total = total + jnp.where(source > to if reverse else source < to, state, 0.0)
                out[r, n, j] = total


def within_kernel(heads, qg_own, qg_other, kv_own, kv_other, weights, attn):
    causal = causal_mask(qg_own.shape[1])
    for n, (qg, kv) in enumerate(((qg_own, kv_own), (qg_other, kv_other))):
        for h in range(heads):
            at = slice(h * DH, (h + 1) * DH)
            w = jnp.where(causal, dot(qg[0, :, at], kv[0, :, at], (1, 1)), 0.0).astype(BF16)
            weights[n, h] = w
            attn[n, :, at] = dot(w, kv[1, :, at], (1, 0))


def forward_kernel(share, r, qg_own, qg_other, within, base, local, grad_sum, att_own, att_other, d_attn, states, every):
    for j in range(share):
        _, at = share_columns(r, j, share)
        to = slice(j * DH, (j + 1) * DH)
        before = base[j].astype(F32)
        total = 0.0
        for n, (qg, out) in enumerate(((qg_own, att_own), (qg_other, att_other))):
            state = (before + local[r, n, j]).astype(BF16)
            states[n, j] = state
            query = qg[0, :, at]
            attn = within[n, :, at] + dot(query, state, (1, 0))
            inverse = 1.0 / jnp.sqrt(jnp.mean(attn * attn, axis=1, keepdims=True) + eps)
            normed = attn * inverse
            out[:, to] = normed.astype(BF16)
            cotangent = qg[1, :, at].astype(F32)
            inner = jnp.mean(cotangent * normed, axis=1, keepdims=True)
            d = ((cotangent - normed * inner) * inverse).astype(BF16)
            d_attn[n, :, to] = d
            grad = dot(query, d, (0, 0))
            every[n, j] = grad.astype(BF16)
            total = total + grad
        grad_sum[j] = total.astype(BF16)


def middle_kernel(share, qg_own, qg_other, kv_own, kv_other, weights, *refs):
    d_attn, states, att_other = refs[:OWNERS], refs[OWNERS : 2 * OWNERS], refs[2 * OWNERS : 3 * OWNERS]
    dq_own, send, key_part, value_part = refs[3 * OWNERS :]
    causal = causal_mask(qg_own.shape[1])
    for r in range(OWNERS):
        for j in range(share):
            head, at = share_columns(r, j, share)
            to = slice(j * DH, (j + 1) * DH)
            send[0, :, at] = att_other[r][:, to]
            for n, (qg, kv) in enumerate(((qg_own, kv_own), (qg_other, kv_other))):
                d = d_attn[r][n, :, to]
                dw = jnp.where(causal, dot(d, kv[1, :, at], (1, 1)), 0.0).astype(BF16)
                d_query = (dot(dw, kv[0, :, at], (1, 0)) + dot(d, states[r][n, j], (1, 1))).astype(BF16)
                if n == 0:
                    dq_own[:, at] = d_query
                else:
                    send[1, :, at] = d_query
                key_part[n, :, at] = dot(dw, qg[0, :, at], (0, 0))
                value_part[n, :, at] = dot(weights[n, head], d, (0, 0))


def final_kernel(share, r, kv_own, kv_other, key_part, value_part, base, local, own, send):
    for j in range(share):
        _, at = share_columns(r, j, share)
        to = slice(j * DH, (j + 1) * DH)
        after = base[j].astype(F32)
        for n, (kv, out) in enumerate(((kv_own, own), (kv_other, send))):
            state = (after + local[r, n, j]).astype(BF16)
            out[0, :, to] = (key_part[n, :, at] + dot(kv[1, :, at], state, (1, 1))).astype(BF16)
            out[1, :, to] = (value_part[n, :, at] + dot(kv[0, :, at], state, (1, 0))).astype(BF16)


def radices(planes):
    bits, found = 1, []
    while bits < planes:
        masks = [bits, 2 * bits, 3 * bits] if 2 * bits < planes else [bits]
        found.append(masks)
        bits *= 4
    return found


def scan(sums, every, reverse, work, later):
    count = lax.axis_size(AXES[0]) * lax.axis_size(AXES[1])
    _, near, _ = pair_bit()
    received = [sums[0]] + [None] * (OWNERS - 1)
    for r in (3, 2, 1):
        received[r] = swap(sums[r], owner_xor(r))
    direct = swap(every, near)
    shape = jax.ShapeDtypeStruct(sums[0].shape, BF16)
    (total,) = call(sum_kernel, received, [shape], grant=4)
    total, later = lax.optimization_barrier((total, later))
    others, steps = [], []
    levels = radices(count // PLANE)
    for level, masks in enumerate(levels):
        got = [swap(total, mask * PLANE) for mask in reversed(masks)]
        others, steps = others + got, steps + masks[::-1]
        if level + 1 < len(levels):
            (total,) = call(sum_kernel, [total, *got], [shape], grant=4)
    done = work(*later)
    others, done = lax.optimization_barrier((others, done))
    mine, across = call(functools.partial(base_kernel, reverse, steps), [*received, *others], [shape] * 2, grant=4)
    (local,) = call(functools.partial(local_kernel, reverse), [every, direct], [jax.ShapeDtypeStruct(every.shape, F32)])
    bases = [mine] + [None] * (OWNERS - 1)
    for r in (3, 2, 1):
        bases[r] = swap(across if r & 2 else mine, owner_xor(r))
    return bases, local, done


def body(queries, key_rows, value_rows, grad_output):
    rows, width = queries.shape
    half = width // 2
    heads = half // DH
    share = heads // OWNERS
    count = lax.axis_size(AXES[0]) * lax.axis_size(AXES[1])
    assert count % PLANE == 0 and count & (count - 1) == 0 and heads % OWNERS == 0
    pair = pair_bit()[0]
    one = 4 * rows * half * DH
    of = jax.ShapeDtypeStruct
    flat, flat_two, wide = of((rows, half), BF16), of((2, rows, half), BF16), of((2, rows, half), F32)
    full = of((rows, width), BF16)
    part, part_two = of((rows, share * DH), BF16), of((2, rows, share * DH), BF16)
    state, state_two = of((share, DH, DH), BF16), of((2, share, DH, DH), BF16)
    state_all = of((OWNERS, 2, share, DH, DH), BF16)
    sems = pltpu.SemaphoreType.DMA

    kv_own, kv_send = call(
        split_kernel, [key_rows, value_rows], [flat_two] * 2, hbm_in=True, scratch=[sems((2, 2))], grant=53
    )
    kv_other = swap(kv_send, pair)
    *sums, every = call(
        functools.partial(states_kernel, share), [kv_own, kv_other], [state] * OWNERS + [state_all], one
    )
    queries, grad_output, *sums = lax.optimization_barrier((queries, grad_output, *sums))
    qg_own, qg_send = call(split_kernel, [queries, grad_output], [flat_two] * 2, hbm_in=True, scratch=[sems((2, 2))])
    qg_other = swap(qg_send, pair)

    def within_work(*operands):
        return call(
            functools.partial(within_kernel, heads), operands, [of((2, heads, rows, rows), BF16), wide], 2 * one
        )

    bases, local, (weights, within) = scan(sums, every, False, within_work, (qg_own, qg_other, kv_own, kv_other))
    results = [None] * OWNERS
    for r in (0, 3, 2, 1):
        results[r] = call(
            functools.partial(forward_kernel, share, r),
            [qg_own, qg_other, within, bases[r], local],
            [state, part, part, part_two, state_two, state_two],
            2 * one // OWNERS,
        )
    grad_sums, att_own, att_other, d_attn, states, grad_every = zip(*results)
    (every,) = call(pack_kernel, grad_every, [state_all])

    def middle_work(*operands):
        return call(functools.partial(middle_kernel, share), operands, [flat, flat_two, wide, wide], 5 * one)

    bases, local, (dq_own, send, key_part, value_part) = scan(
        grad_sums, every, True, middle_work, (qg_own, qg_other, kv_own, kv_other, weights, *d_attn, *states, *att_other)
    )
    attended, grad_queries = call(
        join_first_kernel, [*att_own, dq_own, swap(send, pair)], [full] * 2, hbm_out=True, scratch=[sems((3 + OWNERS,))]
    )
    bases[1], attended, grad_queries = lax.optimization_barrier((bases[1], attended, grad_queries))
    own, received = [None] * OWNERS, [None] * OWNERS
    for r in (0, 3, 2, 1):
        own[r], send = call(
            functools.partial(final_kernel, share, r),
            [kv_own, kv_other, key_part, value_part, bases[r], local],
            [part_two] * 2,
            2 * one // OWNERS,
        )
        received[r] = swap(send, pair)
    grad_keys, grad_values = call(
        join_last_kernel, [*own, *received], [full] * 2, hbm_out=True, scratch=[sems((OWNERS, 2, 2))]
    )
    return (attended, grad_queries, grad_keys, grad_values)


def solution(mesh):
    spec = P(AXES, None)

    return jax.shard_map(body, mesh=mesh, in_specs=(spec,) * 4, out_specs=(spec,) * 4, check_vma=False)
```

profile of v0, /device:TPU:0, one launch (start us, length us, event | category | flops | bytes accessed | tf_op | source)
XLA Modules:
  0.0 71.3 jit_solution(15426390867476325487)
XLA Ops:
  0.6 2.0 %shard_map.75 = (bf16[2,128,1024]{2,1,0:T(8,128)(2,1)S(1)}, bf16[2,128,1024]{2,1,0:T(8,128)(2,1)}) custom-call(bf16[128,2048]{1,0:T(8,128)(2,1)} %a.1, bf16[128,2048]{1,0:T(8,128)(2,1)} %b.1), custom_call_target="tpu_custom_call" | custom-call | bytes 2097152 | tf_op jit(solution)/shard_map/pallas_call | solution.py:59
  2.7 0.6 collective-permute-start
  3.2 1.7 %collective-permute-done.other.kv_other = bf16[2,128,1024]{2,1,0:T(8,128)(2,1)S(1)} collective-permute-done((bf16[2,128,1024]{2,1,0:T(8,128)(2,1)}, bf16[2,128,1024]{2,1,0:T(8,128)(2,1)S(1)}, u32[]{:S(2)}, u32[]{:S(2)}) %collective-permute-start) | collective-permute-done | bytes 524320 | tf_op jit(solution)/shard_map/ppermute | solution.py:52
  5.0 0.5 shard_map.76
  5.5 0.6 copy-done
  6.3 0.4 collective-permute-start.1
  6.7 2.6 %collective-permute-start.8 = (bf16[4,2,2,128,128]{4,3,2,1,0:T(8,128)(2,1)S(1)}, bf16[4,2,2,128,128]{4,3,2,1,0:T(8,128)(2,1)S(1)}, u32[]{:S(2)}, u32[]{:S(2)}) collective-permute-start(bf16[4,2,2,128,128]{4,3,2,1,0:T(8,128)(2,1)S(1)} %get-tuple-element.129.every), channel_id=1, source_target_pairs={{0,1},{1,0},{2,3},{3,2},{4,5},{5,4},{6,7},{7,6},{8,9},{9,8},{10,11... | collective-permute-start | bytes 1572872 | tf_op jit(solution)/shard_map/ppermute | solution.py:52
  9.4 2.0 %collective-permute-start.3 = (bf16[2,128,128]{2,1,0:T(8,128)(2,1)S(1)}, bf16[2,128,128]{2,1,0:T(8,128)(2,1)S(1)}, u32[]{:S(2)}, u32[]{:S(2)}) collective-permute-start(bf16[2,128,128]{2,1,0:T(8,128)(2,1)S(1)} %get-tuple-element.115), channel_id=1, source_target_pairs={{0,4},{1,5},{2,6},{3,7},{4,0},{5,1},{6,2},{7,3},{8,12},{9,13},{10,... | collective-permute-start | bytes 196616 | tf_op jit(solution)/shard_map/ppermute | solution.py:52
  11.4 1.4 %collective-permute-start.4 = (bf16[2,128,128]{2,1,0:T(8,128)(2,1)S(1)}, bf16[2,128,128]{2,1,0:T(8,128)(2,1)S(1)}, u32[]{:S(2)}, u32[]{:S(2)}) collective-permute-start(bf16[2,128,128]{2,1,0:T(8,128)(2,1)S(1)} %get-tuple-element.116), channel_id=1, source_target_pairs={{0,5},{1,4},{2,7},{3,6},{4,1},{5,0},{6,3},{7,2},{8,13},{9,12},{10,... | collective-permute-start | bytes 196616 | tf_op jit(solution)/shard_map/ppermute | solution.py:52
  12.8 10.7 %collective-permute-done.2.refs_1_ = bf16[2,128,128]{2,1,0:T(8,128)(2,1)S(1)} collective-permute-done((bf16[2,128,128]{2,1,0:T(8,128)(2,1)S(1)}, bf16[2,128,128]{2,1,0:T(8,128)(2,1)S(1)}, u32[]{:S(2)}, u32[]{:S(2)}) %collective-permute-start.2) | collective-permute-done | bytes 65568 | tf_op jit(solution)/shard_map/ppermute | solution.py:52
  23.5 2.3 %collective-permute-done.4.refs_3_ = bf16[2,128,128]{2,1,0:T(8,128)(2,1)S(1)} collective-permute-done((bf16[2,128,128]{2,1,0:T(8,128)(2,1)S(1)}, bf16[2,128,128]{2,1,0:T(8,128)(2,1)S(1)}, u32[]{:S(2)}, u32[]{:S(2)}) %collective-permute-start.4) | collective-permute-done | bytes 65568 | tf_op jit(solution)/shard_map/ppermute | solution.py:52
  25.9 1.6 %collective-permute-start.7 = (bf16[2,128,128]{2,1,0:T(8,128)(2,1)S(1)}, bf16[2,128,128]{2,1,0:T(8,128)(2,1)S(1)}, u32[]{:S(2)}, u32[]{:S(2)}) collective-permute-start(bf16[2,128,128]{2,1,0:T(8,128)(2,1)S(1)} %shard_map.78), channel_id=1, source_target_pairs={{0,8},{1,9},{2,10},{3,11},{4,12},{5,13},{6,14},{7,15},{8,0},{9,1},... | collective-permute-start | bytes 196616 | tf_op jit(solution)/shard_map/ppermute | solution.py:52
  27.5 2.6 %collective-permute-start.6 = (bf16[2,128,128]{2,1,0:T(8,128)(2,1)S(1)}, bf16[2,128,128]{2,1,0:T(8,128)(2,1)S(1)}, u32[]{:S(2)}, u32[]{:S(2)}) collective-permute-start(bf16[2,128,128]{2,1,0:T(8,128)(2,1)S(1)} %shard_map.78), channel_id=1, source_target_pairs={{0,16},{1,17},{2,18},{3,19},{4,20},{5,21},{6,22},{7,23},{8,24},{9,... | collective-permute-start | bytes 196616 | tf_op jit(solution)/shard_map/ppermute | solution.py:52
  30.3 2.6 %shard_map.79 = (bf16[2,8,128,128]{3,2,1,0:T(8,128)(2,1)S(1)}, f32[2,128,1024]{2,1,0:T(8,128)S(1)}) custom-call(bf16[2,128,1024]{2,1,0:T(8,128)(2,1)S(1)} %get-tuple-element.149.qg_own, bf16[2,128,1024]{2,1,0:T(8,128)(2,1)S(1)} %collective-permute-done.1.qg_other, bf16[2,128,1024]{2,1,0:T(8,128)(2,1)S(1)} %get-tuple-element.151.own.kv_own, ...), custom_call_target="tpu_custom_call" | custom-call | flops 134217728 | bytes 3670016 | tf_op jit(solution)/shard_map/pallas_call | solution.py:59
  32.9 1.5 %collective-permute-done.6.refs_5_ = bf16[2,128,128]{2,1,0:T(8,128)(2,1)S(1)} collective-permute-done((bf16[2,128,128]{2,1,0:T(8,128)(2,1)S(1)}, bf16[2,128,128]{2,1,0:T(8,128)(2,1)S(1)}, u32[]{:S(2)}, u32[]{:S(2)}) %collective-permute-start.6) | collective-permute-done | bytes 65568 | tf_op jit(solution)/shard_map/ppermute | solution.py:52
  34.5 1.7 %collective-permute-done.5.refs_4_ = bf16[2,128,128]{2,1,0:T(8,128)(2,1)S(1)} collective-permute-done((bf16[2,128,128]{2,1,0:T(8,128)(2,1)S(1)}, bf16[2,128,128]{2,1,0:T(8,128)(2,1)S(1)}, u32[]{:S(2)}, u32[]{:S(2)}) %collective-permute-start.5) | collective-permute-done | bytes 65568 | tf_op jit(solution)/shard_map/ppermute | solution.py:52
  36.3 0.6 collective-permute-start.11
  36.8 2.4 %collective-permute-start.13 = (bf16[2,128,128]{2,1,0:T(8,128)(2,1)S(1)}, bf16[2,128,128]{2,1,0:T(8,128)(2,1)S(1)}, u32[]{:S(2)}, u32[]{:S(2)}) collective-permute-start(bf16[2,128,128]{2,1,0:T(8,128)(2,1)S(1)} %get-tuple-element.132), channel_id=1, source_target_pairs={{0,5},{1,4},{2,7},{3,6},{4,1},{5,0},{6,3},{7,2},{8,13},{9,12},{10,... | collective-permute-start | bytes 196616 | tf_op jit(solution)/shard_map/ppermute | solution.py:52
  39.3 0.5 collective-permute-start.9
  39.8 0.3 shard_map.81.local
  40.1 0.6 collective-permute-done.11.base
  40.7 0.6 shard_map.84
  41.3 0.6 collective-permute-start.12
  42.0 0.6 shard_map.85
  42.6 2.5 %collective-permute-start.14 = (bf16[2,128,128]{2,1,0:T(8,128)(2,1)S(1)}, bf16[2,128,128]{2,1,0:T(8,128)(2,1)S(1)}, u32[]{:S(2)}, u32[]{:S(2)}) collective-permute-start(bf16[2,128,128]{2,1,0:T(8,128)(2,1)S(1)} %get-tuple-element.134), channel_id=1, source_target_pairs={{0,5},{1,4},{2,7},{3,6},{4,1},{5,0},{6,3},{7,2},{8,13},{9,12},{10,... | collective-permute-start | bytes 196616 | tf_op jit(solution)/shard_map/ppermute | solution.py:52
  45.1 0.6 shard_map.83
  45.7 0.6 collective-permute-start.10
  46.3 0.6 shard_map.82
  46.9 0.9 %collective-permute-done.14.refs_3_ = bf16[2,128,128]{2,1,0:T(8,128)(2,1)S(1)} collective-permute-done((bf16[2,128,128]{2,1,0:T(8,128)(2,1)S(1)}, bf16[2,128,128]{2,1,0:T(8,128)(2,1)S(1)}, u32[]{:S(2)}, u32[]{:S(2)}) %collective-permute-start.14) | collective-permute-done | bytes 65568 | tf_op jit(solution)/shard_map/ppermute | solution.py:52
  47.8 2.2 %collective-permute-done.10.refs_1_ = bf16[2,128,128]{2,1,0:T(8,128)(2,1)S(1)} collective-permute-done((bf16[2,128,128]{2,1,0:T(8,128)(2,1)S(1)}, bf16[2,128,128]{2,1,0:T(8,128)(2,1)S(1)}, u32[]{:S(2)}, u32[]{:S(2)}) %collective-permute-start.10) | collective-permute-done | bytes 65568 | tf_op jit(solution)/shard_map/ppermute | solution.py:52
  50.1 2.1 %collective-permute-start.16 = (bf16[2,128,128]{2,1,0:T(8,128)(2,1)S(1)}, bf16[2,128,128]{2,1,0:T(8,128)(2,1)S(1)}, u32[]{:S(2)}, u32[]{:S(2)}) collective-permute-start(bf16[2,128,128]{2,1,0:T(8,128)(2,1)S(1)} %shard_map.86), channel_id=1, source_target_pairs={{0,16},{1,17},{2,18},{3,19},{4,20},{5,21},{6,22},{7,23},{8,24},{9,... | collective-permute-start | bytes 196616 | tf_op jit(solution)/shard_map/ppermute | solution.py:52
  52.2 2.3 %collective-permute-start.15 = (bf16[2,128,128]{2,1,0:T(8,128)(2,1)S(1)}, bf16[2,128,128]{2,1,0:T(8,128)(2,1)S(1)}, u32[]{:S(2)}, u32[]{:S(2)}) collective-permute-start(bf16[2,128,128]{2,1,0:T(8,128)(2,1)S(1)} %shard_map.86), channel_id=1, source_target_pairs={{0,24},{1,25},{2,26},{3,27},{4,28},{5,29},{6,30},{7,31},{8,16},{9,... | collective-permute-start | bytes 196616 | tf_op jit(solution)/shard_map/ppermute | solution.py:52
  54.6 0.6 collective-permute-start.20
  55.2 2.7 %shard_map.87 = (bf16[128,1024]{1,0:T(8,128)(2,1)S(1)}, bf16[2,128,1024]{2,1,0:T(8,128)(2,1)S(1)}, f32[2,128,1024]{2,1,0:T(8,128)S(1)}, f32[2,128,1024]{2,1,0:T(8,128)S(1)}) custom-call(bf16[2,128,1024]{2,1,0:T(8,128)(2,1)S(1)} %get-tuple-element.149.qg_own, bf16[2,128,1024]{2,1,0:T(8,128)(2,1)S(1)} %collective-permute-done.1.qg_other, ...), custom_call_target="tpu_custom_call" | custom-call | flops 335544320 | bytes 6815744 | tf_op jit(solution)/shard_map/pallas_call | solution.py:59
  57.9 0.4 collective-permute-done.15.refs_4_
  58.4 1.1 %collective-permute-start.22 = (bf16[2,128,128]{2,1,0:T(8,128)(2,1)S(1)}, bf16[2,128,128]{2,1,0:T(8,128)(2,1)S(1)}, u32[]{:S(2)}, u32[]{:S(2)}) collective-permute-start(bf16[2,128,128]{2,1,0:T(8,128)(2,1)S(1)} %get-tuple-element.193), channel_id=1, source_target_pairs={{0,5},{1,4},{2,7},{3,6},{4,1},{5,0},{6,3},{7,2},{8,13},{9,12},{10,... | collective-permute-start | bytes 196616 | tf_op jit(solution)/shard_map/ppermute | solution.py:52
  59.6 1.5 %collective-permute-start.21 = (bf16[2,128,128]{2,1,0:T(8,128)(2,1)S(1)}, bf16[2,128,128]{2,1,0:T(8,128)(2,1)S(1)}, u32[]{:S(2)}, u32[]{:S(2)}) collective-permute-start(bf16[2,128,128]{2,1,0:T(8,128)(2,1)S(1)} %get-tuple-element.193), channel_id=1, source_target_pairs={{0,4},{1,5},{2,6},{3,7},{4,0},{5,1},{6,2},{7,3},{8,12},{9,13},{10,... | collective-permute-start | bytes 196616 | tf_op jit(solution)/shard_map/ppermute | solution.py:52
  61.1 0.9 %collective-permute-start.18 = (bf16[2,128,128]{2,1,0:T(8,128)(2,1)S(1)}, bf16[2,128,128]{2,1,0:T(8,128)(2,1)S(1)}, u32[]{:S(2)}, u32[]{:S(2)}) collective-permute-start(bf16[2,128,128]{2,1,0:T(8,128)(2,1)S(1)} %get-tuple-element.173.base), channel_id=1, source_target_pairs={{0,1},{1,0},{2,3},{3,2},{4,5},{5,4},{6,7},{7,6},{8,9},{9,8},{10,11... | collective-permute-start | bytes 196616 | tf_op jit(solution)/shard_map/ppermute | solution.py:52
  62.0 3.2 %collective-permute-done.20.direct = bf16[4,2,2,128,128]{4,3,2,1,0:T(8,128)(2,1)S(1)} collective-permute-done((bf16[4,2,2,128,128]{4,3,2,1,0:T(8,128)(2,1)S(1)}, bf16[4,2,2,128,128]{4,3,2,1,0:T(8,128)(2,1)S(1)}, u32[]{:S(2)}, u32[]{:S(2)}) %collective-permute-start.20) | collective-permute-done | bytes 524320 | tf_op jit(solution)/shard_map/ppermute | solution.py:52
  65.2 0.3 shard_map.91.local
  65.5 0.4 collective-permute-done.22.base
  66.2 0.3 shard_map.94
  66.5 0.6 collective-permute-start.25
  67.4 1.0 %shard_map.89 = (bf16[128,2048]{1,0:T(8,128)(2,1)}, bf16[128,2048]{1,0:T(8,128)(2,1)}) custom-call(bf16[128,256]{1,0:T(8,128)(2,1)S(1)} %get-tuple-element.174.refs_0_, bf16[128,256]{1,0:T(8,128)(2,1)S(1)} %get-tuple-element.175.refs_1_, bf16[128,256]{1,0:T(8,128)(2,1)S(1)} %get-tuple-element.176.refs_2_, bf16[128,256]{1,0:T(8,128)(2,1)S(1)} %get-tuple-element.177.refs_3_, ...), custom_call_target="tpu_custom_call" | custom-call | bytes 2097152 | tf_op jit(solution)/shard_map/pallas_call | solution.py:59
  68.4 0.3 shard_map.93
  68.7 0.5 collective-permute-start.24
  69.2 1.0 %collective-permute-done.24.refs_5_ = bf16[2,128,256]{2,1,0:T(8,128)(2,1)S(1)} collective-permute-done((bf16[2,128,256]{2,1,0:T(8,128)(2,1)S(1)}, bf16[2,128,256]{2,1,0:T(8,128)(2,1)S(1)}, u32[]{:S(2)}, u32[]{:S(2)}) %collective-permute-start.24) | collective-permute-done | bytes 131104 | tf_op jit(solution)/shard_map/ppermute | solution.py:52
  70.2 1.1 %shard_map.96 = (bf16[128,2048]{1,0:T(8,128)(2,1)}, bf16[128,2048]{1,0:T(8,128)(2,1)}) custom-call(bf16[2,128,256]{2,1,0:T(8,128)(2,1)S(1)} %get-tuple-element.190.refs_0_, bf16[2,128,256]{2,1,0:T(8,128)(2,1)S(1)} %get-tuple-element.192.refs_1_, bf16[2,128,256]{2,1,0:T(8,128)(2,1)S(1)} %get-tuple-element.194.refs_2_, ...), custom_call_target="tpu_custom_call" | custom-call | bytes 2097152 | tf_op jit(solution)/shard_map/pallas_call | solution.py:59
  (32 shorter events, 1.7 us)
Async XLA Ops:
  2.7 2.3 %collective-permute-start = (bf16[2,128,1024]{2,1,0:T(8,128)(2,1)}, bf16[2,128,1024]{2,1,0:T(8,128)(2,1)S(1)}, u32[]{:S(2)}, u32[]{:S(2)}) collective-permute-start(bf16[2,128,1024]{2,1,0:T(8,128)(2,1)} %get-tuple-element.104), channel_id=1, source_target_pairs={{0,2},{1,3},{2,0},{3,1},{4,6},{5,7},{6,4},{7,5},{8,10},{9,11},{10,... | collective-permute-start | bytes 1572872 | tf_op jit(solution)/shard_map/ppermute | solution.py:52
  5.0 1.0 %copy-start = (bf16[128,2048]{1,0:T(8,128)(2,1)S(1)}, bf16[128,2048]{1,0:T(8,128)(2,1)}, u32[]{:S(2)}) copy-start(bf16[128,2048]{1,0:T(8,128)(2,1)} %a.2) | copy-start | bytes 1572868
  5.0 1.2 %copy-start.1 = (bf16[128,2048]{1,0:T(8,128)(2,1)S(1)}, bf16[128,2048]{1,0:T(8,128)(2,1)}, u32[]{:S(2)}) copy-start(bf16[128,2048]{1,0:T(8,128)(2,1)} %b.2) | copy-start | bytes 1572868
  6.3 19.6 %collective-permute-start.1 = (bf16[2,128,1024]{2,1,0:T(8,128)(2,1)S(1)}, bf16[2,128,1024]{2,1,0:T(8,128)(2,1)S(1)}, u32[]{:S(2)}, u32[]{:S(2)}) collective-permute-start(bf16[2,128,1024]{2,1,0:T(8,128)(2,1)S(1)} %get-tuple-element.112), channel_id=1, source_target_pairs={{0,2},{1,3},{2,0},{3,1},{4,6},{5,7},{6,4},{7,5},{8,10},{9,11},{10,... | collective-permute-start | bytes 1572872 | tf_op jit(solution)/shard_map/ppermute | solution.py:52
  6.7 33.1 %collective-permute-start.8 = (bf16[4,2,2,128,128]{4,3,2,1,0:T(8,128)(2,1)S(1)}, bf16[4,2,2,128,128]{4,3,2,1,0:T(8,128)(2,1)S(1)}, u32[]{:S(2)}, u32[]{:S(2)}) collective-permute-start(bf16[4,2,2,128,128]{4,3,2,1,0:T(8,128)(2,1)S(1)} %get-tuple-element.129.every), channel_id=1, source_target_pairs={{0,1},{1,0},{2,3},{3,2},{4,5},{5,4},{6,7},{7,6},{8,9},{9,8},{10,11... | collective-permute-start | bytes 1572872 | tf_op jit(solution)/shard_map/ppermute | solution.py:52
  9.3 14.2 %collective-permute-start.2 = (bf16[2,128,128]{2,1,0:T(8,128)(2,1)S(1)}, bf16[2,128,128]{2,1,0:T(8,128)(2,1)S(1)}, u32[]{:S(2)}, u32[]{:S(2)}) collective-permute-start(bf16[2,128,128]{2,1,0:T(8,128)(2,1)S(1)} %get-tuple-element.114), channel_id=1, source_target_pairs={{0,1},{1,0},{2,3},{3,2},{4,5},{5,4},{6,7},{7,6},{8,9},{9,8},{10,11... | collective-permute-start | bytes 196616 | tf_op jit(solution)/shard_map/ppermute | solution.py:52
  9.4 14.2 %collective-permute-start.3 = (bf16[2,128,128]{2,1,0:T(8,128)(2,1)S(1)}, bf16[2,128,128]{2,1,0:T(8,128)(2,1)S(1)}, u32[]{:S(2)}, u32[]{:S(2)}) collective-permute-start(bf16[2,128,128]{2,1,0:T(8,128)(2,1)S(1)} %get-tuple-element.115), channel_id=1, source_target_pairs={{0,4},{1,5},{2,6},{3,7},{4,0},{5,1},{6,2},{7,3},{8,12},{9,13},{10,... | collective-permute-start | bytes 196616 | tf_op jit(solution)/shard_map/ppermute | solution.py:52
  11.4 14.4 %collective-permute-start.4 = (bf16[2,128,128]{2,1,0:T(8,128)(2,1)S(1)}, bf16[2,128,128]{2,1,0:T(8,128)(2,1)S(1)}, u32[]{:S(2)}, u32[]{:S(2)}) collective-permute-start(bf16[2,128,128]{2,1,0:T(8,128)(2,1)S(1)} %get-tuple-element.116), channel_id=1, source_target_pairs={{0,5},{1,4},{2,7},{3,6},{4,1},{5,0},{6,3},{7,2},{8,13},{9,12},{10,... | collective-permute-start | bytes 196616 | tf_op jit(solution)/shard_map/ppermute | solution.py:52
  25.9 7.0 %collective-permute-start.7 = (bf16[2,128,128]{2,1,0:T(8,128)(2,1)S(1)}, bf16[2,128,128]{2,1,0:T(8,128)(2,1)S(1)}, u32[]{:S(2)}, u32[]{:S(2)}) collective-permute-start(bf16[2,128,128]{2,1,0:T(8,128)(2,1)S(1)} %shard_map.78), channel_id=1, source_target_pairs={{0,8},{1,9},{2,10},{3,11},{4,12},{5,13},{6,14},{7,15},{8,0},{9,1},... | collective-permute-start | bytes 196616 | tf_op jit(solution)/shard_map/ppermute | solution.py:52
  27.5 6.9 %collective-permute-start.6 = (bf16[2,128,128]{2,1,0:T(8,128)(2,1)S(1)}, bf16[2,128,128]{2,1,0:T(8,128)(2,1)S(1)}, u32[]{:S(2)}, u32[]{:S(2)}) collective-permute-start(bf16[2,128,128]{2,1,0:T(8,128)(2,1)S(1)} %shard_map.78), channel_id=1, source_target_pairs={{0,16},{1,17},{2,18},{3,19},{4,20},{5,21},{6,22},{7,23},{8,24},{9,... | collective-permute-start | bytes 196616 | tf_op jit(solution)/shard_map/ppermute | solution.py:52
  30.1 6.1 %collective-permute-start.5 = (bf16[2,128,128]{2,1,0:T(8,128)(2,1)S(1)}, bf16[2,128,128]{2,1,0:T(8,128)(2,1)S(1)}, u32[]{:S(2)}, u32[]{:S(2)}) collective-permute-start(bf16[2,128,128]{2,1,0:T(8,128)(2,1)S(1)} %shard_map.78), channel_id=1, source_target_pairs={{0,24},{1,25},{2,26},{3,27},{4,28},{5,29},{6,30},{7,31},{8,16},{9,... | collective-permute-start | bytes 196616 | tf_op jit(solution)/shard_map/ppermute | solution.py:52
  36.3 4.4 %collective-permute-start.11 = (bf16[2,128,128]{2,1,0:T(8,128)(2,1)S(1)}, bf16[2,128,128]{2,1,0:T(8,128)(2,1)S(1)}, u32[]{:S(2)}, u32[]{:S(2)}) collective-permute-start(bf16[2,128,128]{2,1,0:T(8,128)(2,1)S(1)} %get-tuple-element.132), channel_id=1, source_target_pairs={{0,4},{1,5},{2,6},{3,7},{4,0},{5,1},{6,2},{7,3},{8,12},{9,13},{10,... | collective-permute-start | bytes 196616 | tf_op jit(solution)/shard_map/ppermute | solution.py:52
  36.8 5.2 %collective-permute-start.13 = (bf16[2,128,128]{2,1,0:T(8,128)(2,1)S(1)}, bf16[2,128,128]{2,1,0:T(8,128)(2,1)S(1)}, u32[]{:S(2)}, u32[]{:S(2)}) collective-permute-start(bf16[2,128,128]{2,1,0:T(8,128)(2,1)S(1)} %get-tuple-element.132), channel_id=1, source_target_pairs={{0,5},{1,4},{2,7},{3,6},{4,1},{5,0},{6,3},{7,2},{8,13},{9,12},{10,... | collective-permute-start | bytes 196616 | tf_op jit(solution)/shard_map/ppermute | solution.py:52
  39.3 5.8 %collective-permute-start.9 = (bf16[2,128,128]{2,1,0:T(8,128)(2,1)S(1)}, bf16[2,128,128]{2,1,0:T(8,128)(2,1)S(1)}, u32[]{:S(2)}, u32[]{:S(2)}) collective-permute-start(bf16[2,128,128]{2,1,0:T(8,128)(2,1)S(1)} %get-tuple-element.128.base), channel_id=1, source_target_pairs={{0,1},{1,0},{2,3},{3,2},{4,5},{5,4},{6,7},{7,6},{8,9},{9,8},{10,11... | collective-permute-start | bytes 196616 | tf_op jit(solution)/shard_map/ppermute | solution.py:52
  41.3 5.6 %collective-permute-start.12 = (bf16[2,128,128]{2,1,0:T(8,128)(2,1)S(1)}, bf16[2,128,128]{2,1,0:T(8,128)(2,1)S(1)}, u32[]{:S(2)}, u32[]{:S(2)}) collective-permute-start(bf16[2,128,128]{2,1,0:T(8,128)(2,1)S(1)} %get-tuple-element.133), channel_id=1, source_target_pairs={{0,4},{1,5},{2,6},{3,7},{4,0},{5,1},{6,2},{7,3},{8,12},{9,13},{10,... | collective-permute-start | bytes 196616 | tf_op jit(solution)/shard_map/ppermute | solution.py:52
  42.6 5.2 %collective-permute-start.14 = (bf16[2,128,128]{2,1,0:T(8,128)(2,1)S(1)}, bf16[2,128,128]{2,1,0:T(8,128)(2,1)S(1)}, u32[]{:S(2)}, u32[]{:S(2)}) collective-permute-start(bf16[2,128,128]{2,1,0:T(8,128)(2,1)S(1)} %get-tuple-element.134), channel_id=1, source_target_pairs={{0,5},{1,4},{2,7},{3,6},{4,1},{5,0},{6,3},{7,2},{8,13},{9,12},{10,... | collective-permute-start | bytes 196616 | tf_op jit(solution)/shard_map/ppermute | solution.py:52
  45.7 4.3 %collective-permute-start.10 = (bf16[2,128,128]{2,1,0:T(8,128)(2,1)S(1)}, bf16[2,128,128]{2,1,0:T(8,128)(2,1)S(1)}, u32[]{:S(2)}, u32[]{:S(2)}) collective-permute-start(bf16[2,128,128]{2,1,0:T(8,128)(2,1)S(1)} %get-tuple-element.131), channel_id=1, source_target_pairs={{0,1},{1,0},{2,3},{3,2},{4,5},{5,4},{6,7},{7,6},{8,9},{9,8},{10,11... | collective-permute-start | bytes 196616 | tf_op jit(solution)/shard_map/ppermute | solution.py:52
  50.1 7.8 %collective-permute-start.17 = (bf16[2,128,128]{2,1,0:T(8,128)(2,1)S(1)}, bf16[2,128,128]{2,1,0:T(8,128)(2,1)S(1)}, u32[]{:S(2)}, u32[]{:S(2)}) collective-permute-start(bf16[2,128,128]{2,1,0:T(8,128)(2,1)S(1)} %shard_map.86), channel_id=1, source_target_pairs={{0,8},{1,9},{2,10},{3,11},{4,12},{5,13},{6,14},{7,15},{8,0},{9,1},... | collective-permute-start | bytes 196616 | tf_op jit(solution)/shard_map/ppermute | solution.py:52
  50.1 7.7 %collective-permute-start.16 = (bf16[2,128,128]{2,1,0:T(8,128)(2,1)S(1)}, bf16[2,128,128]{2,1,0:T(8,128)(2,1)S(1)}, u32[]{:S(2)}, u32[]{:S(2)}) collective-permute-start(bf16[2,128,128]{2,1,0:T(8,128)(2,1)S(1)} %shard_map.86), channel_id=1, source_target_pairs={{0,16},{1,17},{2,18},{3,19},{4,20},{5,21},{6,22},{7,23},{8,24},{9,... | collective-permute-start | bytes 196616 | tf_op jit(solution)/shard_map/ppermute | solution.py:52
  52.2 6.1 %collective-permute-start.15 = (bf16[2,128,128]{2,1,0:T(8,128)(2,1)S(1)}, bf16[2,128,128]{2,1,0:T(8,128)(2,1)S(1)}, u32[]{:S(2)}, u32[]{:S(2)}) collective-permute-start(bf16[2,128,128]{2,1,0:T(8,128)(2,1)S(1)} %shard_map.86), channel_id=1, source_target_pairs={{0,24},{1,25},{2,26},{3,27},{4,28},{5,29},{6,30},{7,31},{8,16},{9,... | collective-permute-start | bytes 196616 | tf_op jit(solution)/shard_map/ppermute | solution.py:52
  54.6 10.7 %collective-permute-start.20 = (bf16[4,2,2,128,128]{4,3,2,1,0:T(8,128)(2,1)S(1)}, bf16[4,2,2,128,128]{4,3,2,1,0:T(8,128)(2,1)S(1)}, u32[]{:S(2)}, u32[]{:S(2)}) collective-permute-start(bf16[4,2,2,128,128]{4,3,2,1,0:T(8,128)(2,1)S(1)} %shard_map.90.every), channel_id=1, source_target_pairs={{0,1},{1,0},{2,3},{3,2},{4,5},{5,4},{6,7},{7,6},{8,9},{9,8},{10,11... | collective-permute-start | bytes 1572872 | tf_op jit(solution)/shard_map/ppermute | solution.py:52
  58.3 9.0 %collective-permute-start.19 = (bf16[2,128,1024]{2,1,0:T(8,128)(2,1)S(1)}, bf16[2,128,1024]{2,1,0:T(8,128)(2,1)S(1)}, u32[]{:S(2)}, u32[]{:S(2)}) collective-permute-start(bf16[2,128,1024]{2,1,0:T(8,128)(2,1)S(1)} %get-tuple-element.179), channel_id=1, source_target_pairs={{0,2},{1,3},{2,0},{3,1},{4,6},{5,7},{6,4},{7,5},{8,10},{9,11},{10,... | collective-permute-start | bytes 1572872 | tf_op jit(solution)/shard_map/ppermute | solution.py:52
  58.4 7.4 %collective-permute-start.22 = (bf16[2,128,128]{2,1,0:T(8,128)(2,1)S(1)}, bf16[2,128,128]{2,1,0:T(8,128)(2,1)S(1)}, u32[]{:S(2)}, u32[]{:S(2)}) collective-permute-start(bf16[2,128,128]{2,1,0:T(8,128)(2,1)S(1)} %get-tuple-element.193), channel_id=1, source_target_pairs={{0,5},{1,4},{2,7},{3,6},{4,1},{5,0},{6,3},{7,2},{8,13},{9,12},{10,... | collective-permute-start | bytes 196616 | tf_op jit(solution)/shard_map/ppermute | solution.py:52
  59.6 6.6 %collective-permute-start.21 = (bf16[2,128,128]{2,1,0:T(8,128)(2,1)S(1)}, bf16[2,128,128]{2,1,0:T(8,128)(2,1)S(1)}, u32[]{:S(2)}, u32[]{:S(2)}) collective-permute-start(bf16[2,128,128]{2,1,0:T(8,128)(2,1)S(1)} %get-tuple-element.193), channel_id=1, source_target_pairs={{0,4},{1,5},{2,6},{3,7},{4,0},{5,1},{6,2},{7,3},{8,12},{9,13},{10,... | collective-permute-start | bytes 196616 | tf_op jit(solution)/shard_map/ppermute | solution.py:52
  61.1 7.3 %collective-permute-start.18 = (bf16[2,128,128]{2,1,0:T(8,128)(2,1)S(1)}, bf16[2,128,128]{2,1,0:T(8,128)(2,1)S(1)}, u32[]{:S(2)}, u32[]{:S(2)}) collective-permute-start(bf16[2,128,128]{2,1,0:T(8,128)(2,1)S(1)} %get-tuple-element.173.base), channel_id=1, source_target_pairs={{0,1},{1,0},{2,3},{3,2},{4,5},{5,4},{6,7},{7,6},{8,9},{9,8},{10,11... | collective-permute-start | bytes 196616 | tf_op jit(solution)/shard_map/ppermute | solution.py:52
  66.1 3.1 %collective-permute-start.26 = (bf16[2,128,256]{2,1,0:T(8,128)(2,1)S(1)}, bf16[2,128,256]{2,1,0:T(8,128)(2,1)S(1)}, u32[]{:S(2)}, u32[]{:S(2)}) collective-permute-start(bf16[2,128,256]{2,1,0:T(8,128)(2,1)S(1)} %get-tuple-element.199), channel_id=1, source_target_pairs={{0,2},{1,3},{2,0},{3,1},{4,6},{5,7},{6,4},{7,5},{8,10},{9,11},{10,... | collective-permute-start | bytes 393224 | tf_op jit(solution)/shard_map/ppermute | solution.py:52
  66.5 2.7 %collective-permute-start.25 = (bf16[2,128,256]{2,1,0:T(8,128)(2,1)S(1)}, bf16[2,128,256]{2,1,0:T(8,128)(2,1)S(1)}, u32[]{:S(2)}, u32[]{:S(2)}) collective-permute-start(bf16[2,128,256]{2,1,0:T(8,128)(2,1)S(1)} %get-tuple-element.198), channel_id=1, source_target_pairs={{0,2},{1,3},{2,0},{3,1},{4,6},{5,7},{6,4},{7,5},{8,10},{9,11},{10,... | collective-permute-start | bytes 393224 | tf_op jit(solution)/shard_map/ppermute | solution.py:52
  67.3 1.9 %collective-permute-start.23 = (bf16[2,128,256]{2,1,0:T(8,128)(2,1)S(1)}, bf16[2,128,256]{2,1,0:T(8,128)(2,1)S(1)}, u32[]{:S(2)}, u32[]{:S(2)}) collective-permute-start(bf16[2,128,256]{2,1,0:T(8,128)(2,1)S(1)} %get-tuple-element.196), channel_id=1, source_target_pairs={{0,2},{1,3},{2,0},{3,1},{4,6},{5,7},{6,4},{7,5},{8,10},{9,11},{10,... | collective-permute-start | bytes 393224 | tf_op jit(solution)/shard_map/ppermute | solution.py:52
  68.7 1.5 %collective-permute-start.24 = (bf16[2,128,256]{2,1,0:T(8,128)(2,1)S(1)}, bf16[2,128,256]{2,1,0:T(8,128)(2,1)S(1)}, u32[]{:S(2)}, u32[]{:S(2)}) collective-permute-start(bf16[2,128,256]{2,1,0:T(8,128)(2,1)S(1)} %get-tuple-element.197), channel_id=1, source_target_pairs={{0,2},{1,3},{2,0},{3,1},{4,6},{5,7},{6,4},{7,5},{8,10},{9,11},{10,... | collective-permute-start | bytes 393224 | tf_op jit(solution)/shard_map/ppermute | solution.py:52
where the time goes:
time: 71.4 us; the launch traced here: 71.3 us
  starting transfers between devices  28.6 us (40%)
  waiting for transfers between devices  26.9 us (38%)
  Pallas kernels  14.1 us (20%)
  between operations  0.86 us (1%)
  local copies, waits for them, and re-layouts  0.72 us (1%)
    ppermute x27, starting transfers between devices, swap(): return lax.ppermute(x, AXES, [(i, i ^ bits) for i in range(count)])  28.6 us
    ppermute x27, waiting for transfers between devices, swap(): return lax.ppermute(x, AXES, [(i, i ^ bits) for i in range(count)])  26.9 us
    pallas_call x22, Pallas kernels, call(): pl.pallas_call(kernel, out_shape=list(outs), in_specs=[space_in] * len(in...  14.1 us
  transfers between devices with their start and end apart: 27, of which 13 were waited for; matrix products, arithmetic and copies ran while one was open for 0% of the time, Pallas kernels for 15%

commit v1 on v0

--- a/solution.py
+++ b/solution.py
@@ -13,6 +13,7 @@
 PLANE = 8
 GROUP = 4
 OWNERS = 4
+ARRIVAL = (0, 3, 2, 1)
 
 eps = 1e-06
 
@@ -52,16 +53,17 @@
     return lax.ppermute(x, AXES, [(i, i ^ bits) for i in range(count)])
 
 
-def call(kernel, inputs, outs, flops=0, hbm_in=False, hbm_out=False, scratch=(), grant=16):
+def call(kernel, inputs, outs, flops=0, hbm_in=False, hbm_out=False, scratch=(), grant=16, alias=0):
     space_in = pl.BlockSpec(memory_space=pl.ANY if hbm_in else pltpu.VMEM)
     space_out = pl.BlockSpec(memory_space=pl.ANY if hbm_out else pltpu.VMEM)
     moved = sum(a.size * a.dtype.itemsize for a in list(inputs) + list(outs))
     return pl.pallas_call(
         kernel,
         out_shape=list(outs),
-        in_specs=[space_in] * len(inputs),
+        in_specs=[pl.BlockSpec(memory_space=pl.ANY)] * alias + [space_in] * (len(inputs) - alias),
         out_specs=[space_out] * len(outs),
         scratch_shapes=list(scratch),
+        input_output_aliases={n: n for n in range(alias)},
         compiler_params=pltpu.CompilerParams(vmem_limit_bytes=grant * 1024 * 1024),
         cost_estimate=pl.CostEstimate(flops=flops, bytes_accessed=moved, transcendentals=0),
     )(*inputs)
@@ -83,43 +85,60 @@
         copy.wait()
 
 
-def split_kernel(a, b, own, other, sems):
-    half = own.shape[2]
+def half_columns(partner):
     mine = has(pair_bit()[0]).astype(jnp.int32)
+    return 1 - mine if partner else mine
+
+
+def split_kernel(partner, a, b, out, sems):
+    _, rows, half = out.shape
+    chunks = sems.shape[1]
+    at = pl.ds(pl.multiple_of(half_columns(partner) * half, half), half)
     copies = []
-    for k, target in enumerate((other, own)):
+    for k in range(chunks):
+        take = slice(k * rows // chunks, (k + 1) * rows // chunks)
         for n, source in enumerate((a, b)):
-            at = pl.ds(pl.multiple_of((mine if k else 1 - mine) * half, half), half)
-            copies.append(pltpu.make_async_copy(source.at[:, at], target.at[n], sems.at[n, k]))
+            copies.append(pltpu.make_async_copy(source.at[take, at], out.at[n, take], sems.at[n, k]))
     run_copies(copies)
 
 
-def join_first_kernel(*refs):
-    att_own, (dq_own, received), outs, sems = refs[:OWNERS], refs[OWNERS : OWNERS + 2], refs[OWNERS + 2 : -1], refs[-1]
-    half, width = dq_own.shape[1], att_own[0].shape[1]
-    mine = has(pair_bit()[0]).astype(jnp.int32)
-    at = pl.ds(pl.multiple_of((1 - mine) * half, half), half)
-    copies = [pltpu.make_async_copy(received.at[n], outs[n].at[:, at], sems.at[n]) for n in range(2)]
-    at = pl.ds(pl.multiple_of(mine * half, half), half)
-    copies.append(pltpu.make_async_copy(dq_own, outs[1].at[:, at], sems.at[2]))
-    for r in range(OWNERS):
-        at = pl.ds(pl.multiple_of(mine * half + jnp.bitwise_xor(owner(), r) * width, width), width)
-        copies.append(pltpu.make_async_copy(att_own[r], outs[0].at[:, at], sems.at[3 + r]))
+def write_half(source, target, partner, sem):
+    half = source.shape[1]
+    at = pl.ds(pl.multiple_of(half_columns(partner) * half, half), half)
+    return pltpu.make_async_copy(source, target.at[:, at], sem)
+
+
+def write_share(source, target, partner, r, sem):
+    width = source.shape[1]
+    start = (half_columns(partner) * OWNERS + jnp.bitwise_xor(owner(), r)) * width
+    return pltpu.make_async_copy(source, target.at[:, pl.ds(pl.multiple_of(start, width), width)], sem)
+
+
+def join_own_kernel(*refs):
+    att_own, dq_own, (attended, grad_queries), sems = refs[:OWNERS], refs[OWNERS], refs[OWNERS + 1 : -1], refs[-1]
+    copies = [write_half(dq_own, grad_queries, False, sems.at[OWNERS])]
+    copies += [write_share(att_own[r], attended, False, r, sems.at[r]) for r in range(OWNERS)]
     run_copies(copies)
 
 
-def join_last_kernel(*refs):
-    own, received, outs, sems = refs[:OWNERS], refs[OWNERS : 2 * OWNERS], refs[2 * OWNERS : -1], refs[-1]
-    width = own[0].shape[2]
-    half = OWNERS * width
-    mine = has(pair_bit()[0]).astype(jnp.int32)
+def join_most_kernel(count, *refs):
+    swapped, own = refs[2], refs[3 : 3 + OWNERS]
+    received, outs, sems = refs[3 + OWNERS : 3 + OWNERS + count], refs[3 + OWNERS + count : -1], refs[-1]
     copies = []
-    for r in range(OWNERS):
-        for k, sources in enumerate((received, own)):
-            start = (mine if k else 1 - mine) * half + jnp.bitwise_xor(owner(), r) * width
-            for n in range(2):
-                at = pl.ds(pl.multiple_of(start, width), width)
-                copies.append(pltpu.make_async_copy(sources[r].at[n], outs[n].at[:, at], sems.at[r, k, n]))
+    for n in range(2):
+        copies.append(write_half(swapped.at[n], outs[n], True, sems.at[0, n]))
+        for r in range(OWNERS):
+            copies.append(write_share(own[r].at[n], outs[2 + n], False, r, sems.at[1 + r, n]))
+        for k, r in enumerate(ARRIVAL[:count]):
+            copies.append(write_share(received[k].at[n], outs[2 + n], True, r, sems.at[1 + OWNERS + k, n]))
+    run_copies(copies)
+
+
+def join_rest_kernel(count, *refs):
+    received, outs, sems = refs[2 : 2 + OWNERS - count], refs[2 + OWNERS - count : -1], refs[-1]
+    copies = []
+    for k, r in enumerate(ARRIVAL[count:]):
+        copies += [write_share(received[k].at[n], outs[n], True, r, sems.at[k, n]) for n in range(2)]
     run_copies(copies)
 
 
@@ -300,15 +319,32 @@
     state_all = of((OWNERS, 2, share, DH, DH), BF16)
     sems = pltpu.SemaphoreType.DMA
 
-    kv_own, kv_send = call(
-        split_kernel, [key_rows, value_rows], [flat_two] * 2, hbm_in=True, scratch=[sems((2, 2))], grant=53
+    kv_send, kv_own = (
+        call(
+            functools.partial(split_kernel, partner),
+            [key_rows, value_rows],
+            [flat_two],
+            hbm_in=True,
+            scratch=[sems((2, 4))],
+            grant=53,
+        )[0]
+        for partner in (True, False)
     )
     kv_other = swap(kv_send, pair)
     *sums, every = call(
         functools.partial(states_kernel, share), [kv_own, kv_other], [state] * OWNERS + [state_all], one
     )
     queries, grad_output, *sums = lax.optimization_barrier((queries, grad_output, *sums))
-    qg_own, qg_send = call(split_kernel, [queries, grad_output], [flat_two] * 2, hbm_in=True, scratch=[sems((2, 2))])
+    qg_send, qg_own = (
+        call(
+            functools.partial(split_kernel, partner),
+            [queries, grad_output],
+            [flat_two],
+            hbm_in=True,
+            scratch=[sems((2, 1))],
+        )[0]
+        for partner in (True, False)
+    )
     qg_other = swap(qg_send, pair)
 
     def within_work(*operands):
@@ -318,7 +354,7 @@
 
     bases, local, (weights, within) = scan(sums, every, False, within_work, (qg_own, qg_other, kv_own, kv_other))
     results = [None] * OWNERS
-    for r in (0, 3, 2, 1):
+    for r in ARRIVAL:
         results[r] = call(
             functools.partial(forward_kernel, share, r),
             [qg_own, qg_other, within, bases[r], local],
@@ -334,12 +370,12 @@
     bases, local, (dq_own, send, key_part, value_part) = scan(
         grad_sums, every, True, middle_work, (qg_own, qg_other, kv_own, kv_other, weights, *d_attn, *states, *att_other)
     )
+    swapped = swap(send, pair)
     attended, grad_queries = call(
-        join_first_kernel, [*att_own, dq_own, swap(send, pair)], [full] * 2, hbm_out=True, scratch=[sems((3 + OWNERS,))]
-    )
-    bases[1], attended, grad_queries = lax.optimization_barrier((bases[1], attended, grad_queries))
+        join_own_kernel, [*att_own, dq_own], [full] * 2, hbm_out=True, scratch=[sems((OWNERS + 1,))]
+    )
     own, received = [None] * OWNERS, [None] * OWNERS
-    for r in (0, 3, 2, 1):
+    for r in ARRIVAL:
         own[r], send = call(
             functools.partial(final_kernel, share, r),
             [kv_own, kv_other, key_part, value_part, bases[r], local],
@@ -347,8 +383,22 @@
             2 * one // OWNERS,
         )
         received[r] = swap(send, pair)
+    early = OWNERS - 1
+    attended, grad_queries, grad_keys, grad_values = call(
+        functools.partial(join_most_kernel, early),
+        [attended, grad_queries, swapped, *own, *(received[r] for r in ARRIVAL[:early])],
+        [full] * 4,
+        hbm_out=True,
+        scratch=[sems((1 + OWNERS + early, 2))],
+        alias=2,
+    )
     grad_keys, grad_values = call(
-        join_last_kernel, [*own, *received], [full] * 2, hbm_out=True, scratch=[sems((OWNERS, 2, 2))]
+        functools.partial(join_rest_kernel, early),
+        [grad_keys, grad_values, *(received[r] for r in ARRIVAL[early:])],
+        [full] * 2,
+        hbm_out=True,
+        scratch=[sems((OWNERS - early, 2))],
+        alias=2,
     )
     return (attended, grad_queries, grad_keys, grad_values)
 

time: 71.4 us -> 74.9 us (1.049)
  waiting for transfers between devices: 26.9 us -> 30.2 us
  Pallas kernels: 14.1 us -> 15 us
    ppermute x27, waiting for transfers between devices: 26.9 us -> 30.2 us  [swap(): return lax.ppermute(x, AXES, [(i, i ^ bits) for i in range(count)])]
    pallas_call x22 -> x25, Pallas kernels: 14.1 us -> 15 us  [call(): pl.pallas_call(kernel, out_shape=list(outs), in_specs=[pl.BlockSpec(memor...]
  transfers between devices with their start and end apart: 27 -> 27, of which waited for: 13 -> 13; matrix products, arithmetic and copies ran while one was open for 0% -> 0% of each run, Pallas kernels for 15% -> 16%
where the time goes in v1:
time: 74.9 us; the launch traced here: 74.7 us
  waiting for transfers between devices  30.2 us (40%)
  starting transfers between devices  28.2 us (38%)
  Pallas kernels  15 us (20%)
  between operations  0.92 us (1%)
    ppermute x27, waiting for transfers between devices, swap(): return lax.ppermute(x, AXES, [(i, i ^ bits) for i in range(count)])  30.2 us
    ppermute x27, starting transfers between devices, swap(): return lax.ppermute(x, AXES, [(i, i ^ bits) for i in range(count)])  28.2 us
    pallas_call x25, Pallas kernels, call(): pl.pallas_call(kernel, out_shape=list(outs), in_specs=[pl.BlockSpec(memor...  15 us
  transfers between devices with their start and end apart: 27, of which 13 were waited for; matrix products, arithmetic and copies ran while one was open for 0% of the time, Pallas kernels for 16%

profile of v1, /device:TPU:0, one launch (start us, length us, event | category | flops | bytes accessed | tf_op | source)
XLA Modules:
  0.0 74.7 jit_solution(13207125672662595330)
XLA Ops:
  0.6 1.1 %shard_map.76 = bf16[2,128,1024]{2,1,0:T(8,128)(2,1)S(1)} custom-call(bf16[128,2048]{1,0:T(8,128)(2,1)} %a.3, bf16[128,2048]{1,0:T(8,128)(2,1)} %b.3), custom_call_target="tpu_custom_call" | custom-call | bytes 1572864 | tf_op jit(solution)/shard_map/pallas_call | solution.py:60
  1.8 0.6 collective-permute-start
  2.3 1.1 %shard_map.75.own.kv_own = bf16[2,128,1024]{2,1,0:T(8,128)(2,1)S(1)} custom-call(bf16[128,2048]{1,0:T(8,128)(2,1)} %a.3, bf16[128,2048]{1,0:T(8,128)(2,1)} %b.3), custom_call_target="tpu_custom_call" | custom-call | bytes 1572864 | tf_op jit(solution)/shard_map/pallas_call | solution.py:60
  3.5 0.4 collective-permute-done.other.kv_other
  3.9 0.5 shard_map.77
  4.9 2.9 %collective-permute-start.8 = (bf16[4,2,2,128,128]{4,3,2,1,0:T(8,128)(2,1)S(1)}, bf16[4,2,2,128,128]{4,3,2,1,0:T(8,128)(2,1)S(1)}, u32[]{:S(2)}, u32[]{:S(2)}) collective-permute-start(bf16[4,2,2,128,128]{4,3,2,1,0:T(8,128)(2,1)S(1)} %get-tuple-element.122.every), channel_id=1, source_target_pairs={{0,1},{1,0},{2,3},{3,2},{4,5},{5,4},{6,7},{7,6},{8,9},{9,8},{10,11... | collective-permute-start | bytes 1572872 | tf_op jit(solution)/shard_map/ppermute | solution.py:53
  7.8 2.0 %collective-permute-start.3 = (bf16[2,128,128]{2,1,0:T(8,128)(2,1)S(1)}, bf16[2,128,128]{2,1,0:T(8,128)(2,1)S(1)}, u32[]{:S(2)}, u32[]{:S(2)}) collective-permute-start(bf16[2,128,128]{2,1,0:T(8,128)(2,1)S(1)} %get-tuple-element.108), channel_id=1, source_target_pairs={{0,4},{1,5},{2,6},{3,7},{4,0},{5,1},{6,2},{7,3},{8,12},{9,13},{10,... | collective-permute-start | bytes 196616 | tf_op jit(solution)/shard_map/ppermute | solution.py:53
  9.9 1.4 %collective-permute-start.4 = (bf16[2,128,128]{2,1,0:T(8,128)(2,1)S(1)}, bf16[2,128,128]{2,1,0:T(8,128)(2,1)S(1)}, u32[]{:S(2)}, u32[]{:S(2)}) collective-permute-start(bf16[2,128,128]{2,1,0:T(8,128)(2,1)S(1)} %get-tuple-element.109), channel_id=1, source_target_pairs={{0,5},{1,4},{2,7},{3,6},{4,1},{5,0},{6,3},{7,2},{8,13},{9,12},{10,... | collective-permute-start | bytes 196616 | tf_op jit(solution)/shard_map/ppermute | solution.py:53
  11.4 10.6 %collective-permute-done.2.refs_1_ = bf16[2,128,128]{2,1,0:T(8,128)(2,1)S(1)} collective-permute-done((bf16[2,128,128]{2,1,0:T(8,128)(2,1)S(1)}, bf16[2,128,128]{2,1,0:T(8,128)(2,1)S(1)}, u32[]{:S(2)}, u32[]{:S(2)}) %collective-permute-start.2) | collective-permute-done | bytes 65568 | tf_op jit(solution)/shard_map/ppermute | solution.py:53
  22.0 2.0 %collective-permute-done.4.refs_3_ = bf16[2,128,128]{2,1,0:T(8,128)(2,1)S(1)} collective-permute-done((bf16[2,128,128]{2,1,0:T(8,128)(2,1)S(1)}, bf16[2,128,128]{2,1,0:T(8,128)(2,1)S(1)}, u32[]{:S(2)}, u32[]{:S(2)}) %collective-permute-start.4) | collective-permute-done | bytes 65568 | tf_op jit(solution)/shard_map/ppermute | solution.py:53
  24.0 1.6 %collective-permute-start.7 = (bf16[2,128,128]{2,1,0:T(8,128)(2,1)S(1)}, bf16[2,128,128]{2,1,0:T(8,128)(2,1)S(1)}, u32[]{:S(2)}, u32[]{:S(2)}) collective-permute-start(bf16[2,128,128]{2,1,0:T(8,128)(2,1)S(1)} %shard_map.80), channel_id=1, source_target_pairs={{0,8},{1,9},{2,10},{3,11},{4,12},{5,13},{6,14},{7,15},{8,0},{9,1},... | collective-permute-start | bytes 196616 | tf_op jit(solution)/shard_map/ppermute | solution.py:53
  25.7 2.6 %collective-permute-start.6 = (bf16[2,128,128]{2,1,0:T(8,128)(2,1)S(1)}, bf16[2,128,128]{2,1,0:T(8,128)(2,1)S(1)}, u32[]{:S(2)}, u32[]{:S(2)}) collective-permute-start(bf16[2,128,128]{2,1,0:T(8,128)(2,1)S(1)} %shard_map.80), channel_id=1, source_target_pairs={{0,16},{1,17},{2,18},{3,19},{4,20},{5,21},{6,22},{7,23},{8,24},{9,... | collective-permute-start | bytes 196616 | tf_op jit(solution)/shard_map/ppermute | solution.py:53
  28.5 2.6 %shard_map.81 = (bf16[2,8,128,128]{3,2,1,0:T(8,128)(2,1)S(1)}, f32[2,128,1024]{2,1,0:T(8,128)S(1)}) custom-call(bf16[2,128,1024]{2,1,0:T(8,128)(2,1)S(1)} %shard_map.78.qg_own, bf16[2,128,1024]{2,1,0:T(8,128)(2,1)S(1)} %collective-permute-done.1.qg_other, bf16[2,128,1024]{2,1,0:T(8,128)(2,1)S(1)} %shard_map.75.own.kv_own, ...), custom_call_target="tpu_custom_call" | custom-call | flops 134217728 | bytes 3670016 | tf_op jit(solution)/shard_map/pallas_call | solution.py:60
  31.1 1.2 %collective-permute-done.6.refs_5_ = bf16[2,128,128]{2,1,0:T(8,128)(2,1)S(1)} collective-permute-done((bf16[2,128,128]{2,1,0:T(8,128)(2,1)S(1)}, bf16[2,128,128]{2,1,0:T(8,128)(2,1)S(1)}, u32[]{:S(2)}, u32[]{:S(2)}) %collective-permute-start.6) | collective-permute-done | bytes 65568 | tf_op jit(solution)/shard_map/ppermute | solution.py:53
  32.2 2.1 %collective-permute-done.5.refs_4_ = bf16[2,128,128]{2,1,0:T(8,128)(2,1)S(1)} collective-permute-done((bf16[2,128,128]{2,1,0:T(8,128)(2,1)S(1)}, bf16[2,128,128]{2,1,0:T(8,128)(2,1)S(1)}, u32[]{:S(2)}, u32[]{:S(2)}) %collective-permute-start.5) | collective-permute-done | bytes 65568 | tf_op jit(solution)/shard_map/ppermute | solution.py:53
  34.4 0.6 collective-permute-start.10
  35.0 2.4 %collective-permute-start.11 = (bf16[2,128,128]{2,1,0:T(8,128)(2,1)S(1)}, bf16[2,128,128]{2,1,0:T(8,128)(2,1)S(1)}, u32[]{:S(2)}, u32[]{:S(2)}) collective-permute-start(bf16[2,128,128]{2,1,0:T(8,128)(2,1)S(1)} %get-tuple-element.125), channel_id=1, source_target_pairs={{0,5},{1,4},{2,7},{3,6},{4,1},{5,0},{6,3},{7,2},{8,13},{9,12},{10,... | collective-permute-start | bytes 196616 | tf_op jit(solution)/shard_map/ppermute | solution.py:53
  37.4 0.5 collective-permute-start.9
  38.0 0.3 shard_map.83.local
  38.3 0.6 shard_map.84
  38.9 0.6 shard_map.86
  39.4 0.7 collective-permute-done.11.base
  40.2 0.6 shard_map.87
  40.8 1.7 %collective-permute-done.9.base = bf16[2,128,128]{2,1,0:T(8,128)(2,1)S(1)} collective-permute-done((bf16[2,128,128]{2,1,0:T(8,128)(2,1)S(1)}, bf16[2,128,128]{2,1,0:T(8,128)(2,1)S(1)}, u32[]{:S(2)}, u32[]{:S(2)}) %collective-permute-start.9) | collective-permute-done | bytes 65568 | tf_op jit(solution)/shard_map/ppermute | solution.py:53
  42.4 0.6 shard_map.85
  43.0 0.8 %collective-permute-start.19 = (bf16[4,2,2,128,128]{4,3,2,1,0:T(8,128)(2,1)S(1)}, bf16[4,2,2,128,128]{4,3,2,1,0:T(8,128)(2,1)S(1)}, u32[]{:S(2)}, u32[]{:S(2)}) collective-permute-start(bf16[4,2,2,128,128]{4,3,2,1,0:T(8,128)(2,1)S(1)} %shard_map.92.every), channel_id=1, source_target_pairs={{0,1},{1,0},{2,3},{3,2},{4,5},{5,4},{6,7},{7,6},{8,9},{9,8},{10,11... | collective-permute-start | bytes 1572872 | tf_op jit(solution)/shard_map/ppermute | solution.py:53
  43.9 0.7 collective-permute-start.13
  44.5 2.1 %collective-permute-start.14 = (bf16[2,128,128]{2,1,0:T(8,128)(2,1)S(1)}, bf16[2,128,128]{2,1,0:T(8,128)(2,1)S(1)}, u32[]{:S(2)}, u32[]{:S(2)}) collective-permute-start(bf16[2,128,128]{2,1,0:T(8,128)(2,1)S(1)} %get-tuple-element.131), channel_id=1, source_target_pairs={{0,5},{1,4},{2,7},{3,6},{4,1},{5,0},{6,3},{7,2},{8,13},{9,12},{10,... | collective-permute-start | bytes 196616 | tf_op jit(solution)/shard_map/ppermute | solution.py:53
  46.6 0.7 collective-permute-start.12
  47.3 0.9 %collective-permute-done.13.refs_2_ = bf16[2,128,128]{2,1,0:T(8,128)(2,1)S(1)} collective-permute-done((bf16[2,128,128]{2,1,0:T(8,128)(2,1)S(1)}, bf16[2,128,128]{2,1,0:T(8,128)(2,1)S(1)}, u32[]{:S(2)}, u32[]{:S(2)}) %collective-permute-start.13) | collective-permute-done | bytes 65568 | tf_op jit(solution)/shard_map/ppermute | solution.py:53
  48.3 6.7 %collective-permute-done.14.refs_3_ = bf16[2,128,128]{2,1,0:T(8,128)(2,1)S(1)} collective-permute-done((bf16[2,128,128]{2,1,0:T(8,128)(2,1)S(1)}, bf16[2,128,128]{2,1,0:T(8,128)(2,1)S(1)}, u32[]{:S(2)}, u32[]{:S(2)}) %collective-permute-start.14) | collective-permute-done | bytes 65568 | tf_op jit(solution)/shard_map/ppermute | solution.py:53
  55.0 0.4 collective-permute-done.12.refs_1_
  55.5 1.8 %collective-permute-start.16 = (bf16[2,128,128]{2,1,0:T(8,128)(2,1)S(1)}, bf16[2,128,128]{2,1,0:T(8,128)(2,1)S(1)}, u32[]{:S(2)}, u32[]{:S(2)}) collective-permute-start(bf16[2,128,128]{2,1,0:T(8,128)(2,1)S(1)} %shard_map.88), channel_id=1, source_target_pairs={{0,16},{1,17},{2,18},{3,19},{4,20},{5,21},{6,22},{7,23},{8,24},{9,... | collective-permute-start | bytes 196616 | tf_op jit(solution)/shard_map/ppermute | solution.py:53
  57.3 2.6 %collective-permute-start.15 = (bf16[2,128,128]{2,1,0:T(8,128)(2,1)S(1)}, bf16[2,128,128]{2,1,0:T(8,128)(2,1)S(1)}, u32[]{:S(2)}, u32[]{:S(2)}) collective-permute-start(bf16[2,128,128]{2,1,0:T(8,128)(2,1)S(1)} %shard_map.88), channel_id=1, source_target_pairs={{0,24},{1,25},{2,26},{3,27},{4,28},{5,29},{6,30},{7,31},{8,16},{9,... | collective-permute-start | bytes 196616 | tf_op jit(solution)/shard_map/ppermute | solution.py:53
  59.9 2.7 %shard_map.89 = (bf16[128,1024]{1,0:T(8,128)(2,1)S(1)}, bf16[2,128,1024]{2,1,0:T(8,128)(2,1)S(1)}, f32[2,128,1024]{2,1,0:T(8,128)S(1)}, f32[2,128,1024]{2,1,0:T(8,128)S(1)}) custom-call(bf16[2,128,1024]{2,1,0:T(8,128)(2,1)S(1)} %shard_map.78.qg_own, bf16[2,128,1024]{2,1,0:T(8,128)(2,1)S(1)} %collective-permute-done.1.qg_other, ...), custom_call_target="tpu_custom_call" | custom-call | flops 335544320 | bytes 6815744 | tf_op jit(solution)/shard_map/pallas_call | solution.py:60
  62.6 0.8 %collective-permute-done.15.refs_4_ = bf16[2,128,128]{2,1,0:T(8,128)(2,1)S(1)} collective-permute-done((bf16[2,128,128]{2,1,0:T(8,128)(2,1)S(1)}, bf16[2,128,128]{2,1,0:T(8,128)(2,1)S(1)}, u32[]{:S(2)}, u32[]{:S(2)}) %collective-permute-start.15) | collective-permute-done | bytes 65568 | tf_op jit(solution)/shard_map/ppermute | solution.py:53
  63.5 1.2 %collective-permute-start.22 = (bf16[2,128,128]{2,1,0:T(8,128)(2,1)S(1)}, bf16[2,128,128]{2,1,0:T(8,128)(2,1)S(1)}, u32[]{:S(2)}, u32[]{:S(2)}) collective-permute-start(bf16[2,128,128]{2,1,0:T(8,128)(2,1)S(1)} %get-tuple-element.183), channel_id=1, source_target_pairs={{0,5},{1,4},{2,7},{3,6},{4,1},{5,0},{6,3},{7,2},{8,13},{9,12},{10,... | collective-permute-start | bytes 196616 | tf_op jit(solution)/shard_map/ppermute | solution.py:53
  64.7 1.0 %collective-permute-start.21 = (bf16[2,128,128]{2,1,0:T(8,128)(2,1)S(1)}, bf16[2,128,128]{2,1,0:T(8,128)(2,1)S(1)}, u32[]{:S(2)}, u32[]{:S(2)}) collective-permute-start(bf16[2,128,128]{2,1,0:T(8,128)(2,1)S(1)} %get-tuple-element.183), channel_id=1, source_target_pairs={{0,4},{1,5},{2,6},{3,7},{4,0},{5,1},{6,2},{7,3},{8,12},{9,13},{10,... | collective-permute-start | bytes 196616 | tf_op jit(solution)/shard_map/ppermute | solution.py:53
  65.7 1.3 %collective-permute-start.20 = (bf16[2,128,128]{2,1,0:T(8,128)(2,1)S(1)}, bf16[2,128,128]{2,1,0:T(8,128)(2,1)S(1)}, u32[]{:S(2)}, u32[]{:S(2)}) collective-permute-start(bf16[2,128,128]{2,1,0:T(8,128)(2,1)S(1)} %get-tuple-element.176.base), channel_id=1, source_target_pairs={{0,1},{1,0},{2,3},{3,2},{4,5},{5,4},{6,7},{7,6},{8,9},{9,8},{10,11... | collective-permute-start | bytes 196616 | tf_op jit(solution)/shard_map/ppermute | solution.py:53
  67.1 0.3 shard_map.93.local
  67.3 2.0 %collective-permute-done.22.base = bf16[2,128,128]{2,1,0:T(8,128)(2,1)S(1)} collective-permute-done((bf16[2,128,128]{2,1,0:T(8,128)(2,1)S(1)}, bf16[2,128,128]{2,1,0:T(8,128)(2,1)S(1)}, u32[]{:S(2)}, u32[]{:S(2)}) %collective-permute-start.22) | collective-permute-done | bytes 65568 | tf_op jit(solution)/shard_map/ppermute | solution.py:53
  69.7 0.7 collective-permute-done.21.base
  70.3 0.3 shard_map.96
  70.9 0.6 collective-permute-start.23
  71.5 0.2 shard_map.95
  71.8 0.8 %shard_map.90 = (bf16[128,2048]{1,0:T(8,128)(2,1)}, bf16[128,2048]{1,0:T(8,128)(2,1)}) custom-call(bf16[128,256]{1,0:T(8,128)(2,1)S(1)} %get-tuple-element.123.refs_0_, bf16[128,256]{1,0:T(8,128)(2,1)S(1)} %get-tuple-element.124.refs_1_, bf16[128,256]{1,0:T(8,128)(2,1)S(1)} %get-tuple-element.126.refs_2_, bf16[128,256]{1,0:T(8,128)(2,1)S(1)} %get-tuple-element.127.refs_3_, ...), custom_call_target="tpu_custom_call" | custom-call | bytes 1572864 | tf_op jit(solution)/shard_map/pallas_call | solution.py:60
  72.7 1.2 %shard_map.98 = (bf16[128,2048]{1,0:T(8,128)(2,1)}, bf16[128,2048]{1,0:T(8,128)(2,1)}, bf16[128,2048]{1,0:T(8,128)(2,1)}, bf16[128,2048]{1,0:T(8,128)(2,1)}) custom-call(bf16[128,2048]{1,0:T(8,128)(2,1)} %get-tuple-element.168.refs_0_, bf16[128,2048]{1,0:T(8,128)(2,1)} %get-tuple-element.169.refs_1_, ...), custom_call_target="tpu_custom_call", output_to_operand_aliasing={{0}: (0, {}), {1}: (1, {})} | custom-call | bytes 4587520 | tf_op jit(solution)/shard_map/pallas_call | solution.py:60
  74.0 0.7 shard_map.99
  (35 shorter events, 2.0 us)
Async XLA Ops:
  1.8 2.1 %collective-permute-start = (bf16[2,128,1024]{2,1,0:T(8,128)(2,1)S(1)}, bf16[2,128,1024]{2,1,0:T(8,128)(2,1)S(1)}, u32[]{:S(2)}, u32[]{:S(2)}) collective-permute-start(bf16[2,128,1024]{2,1,0:T(8,128)(2,1)S(1)} %shard_map.76), channel_id=1, source_target_pairs={{0,2},{1,3},{2,0},{3,1},{4,6},{5,7},{6,4},{7,5},{8,10},{9,11},{10,... | collective-permute-start | bytes 1572872 | tf_op jit(solution)/shard_map/ppermute | solution.py:53
  3.5 1.0 %copy-start = (bf16[128,2048]{1,0:T(8,128)(2,1)S(1)}, bf16[128,2048]{1,0:T(8,128)(2,1)}, u32[]{:S(2)}) copy-start(bf16[128,2048]{1,0:T(8,128)(2,1)} %a.5) | copy-start | bytes 1572868
  3.5 1.2 %copy-start.1 = (bf16[128,2048]{1,0:T(8,128)(2,1)S(1)}, bf16[128,2048]{1,0:T(8,128)(2,1)}, u32[]{:S(2)}) copy-start(bf16[128,2048]{1,0:T(8,128)(2,1)} %b.5) | copy-start | bytes 1572868
  4.7 19.3 %collective-permute-start.1 = (bf16[2,128,1024]{2,1,0:T(8,128)(2,1)S(1)}, bf16[2,128,1024]{2,1,0:T(8,128)(2,1)S(1)}, u32[]{:S(2)}, u32[]{:S(2)}) collective-permute-start(bf16[2,128,1024]{2,1,0:T(8,128)(2,1)S(1)} %shard_map.79), channel_id=1, source_target_pairs={{0,2},{1,3},{2,0},{3,1},{4,6},{5,7},{6,4},{7,5},{8,10},{9,11},{10,... | collective-permute-start | bytes 1572872 | tf_op jit(solution)/shard_map/ppermute | solution.py:53
  4.9 33.1 %collective-permute-start.8 = (bf16[4,2,2,128,128]{4,3,2,1,0:T(8,128)(2,1)S(1)}, bf16[4,2,2,128,128]{4,3,2,1,0:T(8,128)(2,1)S(1)}, u32[]{:S(2)}, u32[]{:S(2)}) collective-permute-start(bf16[4,2,2,128,128]{4,3,2,1,0:T(8,128)(2,1)S(1)} %get-tuple-element.122.every), channel_id=1, source_target_pairs={{0,1},{1,0},{2,3},{3,2},{4,5},{5,4},{6,7},{7,6},{8,9},{9,8},{10,11... | collective-permute-start | bytes 1572872 | tf_op jit(solution)/shard_map/ppermute | solution.py:53
  7.8 14.2 %collective-permute-start.2 = (bf16[2,128,128]{2,1,0:T(8,128)(2,1)S(1)}, bf16[2,128,128]{2,1,0:T(8,128)(2,1)S(1)}, u32[]{:S(2)}, u32[]{:S(2)}) collective-permute-start(bf16[2,128,128]{2,1,0:T(8,128)(2,1)S(1)} %get-tuple-element.107), channel_id=1, source_target_pairs={{0,1},{1,0},{2,3},{3,2},{4,5},{5,4},{6,7},{7,6},{8,9},{9,8},{10,11... | collective-permute-start | bytes 196616 | tf_op jit(solution)/shard_map/ppermute | solution.py:53
  7.8 14.2 %collective-permute-start.3 = (bf16[2,128,128]{2,1,0:T(8,128)(2,1)S(1)}, bf16[2,128,128]{2,1,0:T(8,128)(2,1)S(1)}, u32[]{:S(2)}, u32[]{:S(2)}) collective-permute-start(bf16[2,128,128]{2,1,0:T(8,128)(2,1)S(1)} %get-tuple-element.108), channel_id=1, source_target_pairs={{0,4},{1,5},{2,6},{3,7},{4,0},{5,1},{6,2},{7,3},{8,12},{9,13},{10,... | collective-permute-start | bytes 196616 | tf_op jit(solution)/shard_map/ppermute | solution.py:53
  9.9 14.1 %collective-permute-start.4 = (bf16[2,128,128]{2,1,0:T(8,128)(2,1)S(1)}, bf16[2,128,128]{2,1,0:T(8,128)(2,1)S(1)}, u32[]{:S(2)}, u32[]{:S(2)}) collective-permute-start(bf16[2,128,128]{2,1,0:T(8,128)(2,1)S(1)} %get-tuple-element.109), channel_id=1, source_target_pairs={{0,5},{1,4},{2,7},{3,6},{4,1},{5,0},{6,3},{7,2},{8,13},{9,12},{10,... | collective-permute-start | bytes 196616 | tf_op jit(solution)/shard_map/ppermute | solution.py:53
  24.0 7.0 %collective-permute-start.7 = (bf16[2,128,128]{2,1,0:T(8,128)(2,1)S(1)}, bf16[2,128,128]{2,1,0:T(8,128)(2,1)S(1)}, u32[]{:S(2)}, u32[]{:S(2)}) collective-permute-start(bf16[2,128,128]{2,1,0:T(8,128)(2,1)S(1)} %shard_map.80), channel_id=1, source_target_pairs={{0,8},{1,9},{2,10},{3,11},{4,12},{5,13},{6,14},{7,15},{8,0},{9,1},... | collective-permute-start | bytes 196616 | tf_op jit(solution)/shard_map/ppermute | solution.py:53
  25.7 6.6 %collective-permute-start.6 = (bf16[2,128,128]{2,1,0:T(8,128)(2,1)S(1)}, bf16[2,128,128]{2,1,0:T(8,128)(2,1)S(1)}, u32[]{:S(2)}, u32[]{:S(2)}) collective-permute-start(bf16[2,128,128]{2,1,0:T(8,128)(2,1)S(1)} %shard_map.80), channel_id=1, source_target_pairs={{0,16},{1,17},{2,18},{3,19},{4,20},{5,21},{6,22},{7,23},{8,24},{9,... | collective-permute-start | bytes 196616 | tf_op jit(solution)/shard_map/ppermute | solution.py:53
  28.3 6.1 %collective-permute-start.5 = (bf16[2,128,128]{2,1,0:T(8,128)(2,1)S(1)}, bf16[2,128,128]{2,1,0:T(8,128)(2,1)S(1)}, u32[]{:S(2)}, u32[]{:S(2)}) collective-permute-start(bf16[2,128,128]{2,1,0:T(8,128)(2,1)S(1)} %shard_map.80), channel_id=1, source_target_pairs={{0,24},{1,25},{2,26},{3,27},{4,28},{5,29},{6,30},{7,31},{8,16},{9,... | collective-permute-start | bytes 196616 | tf_op jit(solution)/shard_map/ppermute | solution.py:53
  34.4 4.4 %collective-permute-start.10 = (bf16[2,128,128]{2,1,0:T(8,128)(2,1)S(1)}, bf16[2,128,128]{2,1,0:T(8,128)(2,1)S(1)}, u32[]{:S(2)}, u32[]{:S(2)}) collective-permute-start(bf16[2,128,128]{2,1,0:T(8,128)(2,1)S(1)} %get-tuple-element.125), channel_id=1, source_target_pairs={{0,4},{1,5},{2,6},{3,7},{4,0},{5,1},{6,2},{7,3},{8,12},{9,13},{10,... | collective-permute-start | bytes 196616 | tf_op jit(solution)/shard_map/ppermute | solution.py:53
  35.0 5.2 %collective-permute-start.11 = (bf16[2,128,128]{2,1,0:T(8,128)(2,1)S(1)}, bf16[2,128,128]{2,1,0:T(8,128)(2,1)S(1)}, u32[]{:S(2)}, u32[]{:S(2)}) collective-permute-start(bf16[2,128,128]{2,1,0:T(8,128)(2,1)S(1)} %get-tuple-element.125), channel_id=1, source_target_pairs={{0,5},{1,4},{2,7},{3,6},{4,1},{5,0},{6,3},{7,2},{8,13},{9,12},{10,... | collective-permute-start | bytes 196616 | tf_op jit(solution)/shard_map/ppermute | solution.py:53
  37.4 5.0 %collective-permute-start.9 = (bf16[2,128,128]{2,1,0:T(8,128)(2,1)S(1)}, bf16[2,128,128]{2,1,0:T(8,128)(2,1)S(1)}, u32[]{:S(2)}, u32[]{:S(2)}) collective-permute-start(bf16[2,128,128]{2,1,0:T(8,128)(2,1)S(1)} %get-tuple-element.121.base), channel_id=1, source_target_pairs={{0,1},{1,0},{2,3},{3,2},{4,5},{5,4},{6,7},{7,6},{8,9},{9,8},{10,11... | collective-permute-start | bytes 196616 | tf_op jit(solution)/shard_map/ppermute | solution.py:53
  43.0 24.0 %collective-permute-start.19 = (bf16[4,2,2,128,128]{4,3,2,1,0:T(8,128)(2,1)S(1)}, bf16[4,2,2,128,128]{4,3,2,1,0:T(8,128)(2,1)S(1)}, u32[]{:S(2)}, u32[]{:S(2)}) collective-permute-start(bf16[4,2,2,128,128]{4,3,2,1,0:T(8,128)(2,1)S(1)} %shard_map.92.every), channel_id=1, source_target_pairs={{0,1},{1,0},{2,3},{3,2},{4,5},{5,4},{6,7},{7,6},{8,9},{9,8},{10,11... | collective-permute-start | bytes 1572872 | tf_op jit(solution)/shard_map/ppermute | solution.py:53
  43.9 4.4 %collective-permute-start.13 = (bf16[2,128,128]{2,1,0:T(8,128)(2,1)S(1)}, bf16[2,128,128]{2,1,0:T(8,128)(2,1)S(1)}, u32[]{:S(2)}, u32[]{:S(2)}) collective-permute-start(bf16[2,128,128]{2,1,0:T(8,128)(2,1)S(1)} %get-tuple-element.130), channel_id=1, source_target_pairs={{0,4},{1,5},{2,6},{3,7},{4,0},{5,1},{6,2},{7,3},{8,12},{9,13},{10,... | collective-permute-start | bytes 196616 | tf_op jit(solution)/shard_map/ppermute | solution.py:53
  44.5 10.5 %collective-permute-start.14 = (bf16[2,128,128]{2,1,0:T(8,128)(2,1)S(1)}, bf16[2,128,128]{2,1,0:T(8,128)(2,1)S(1)}, u32[]{:S(2)}, u32[]{:S(2)}) collective-permute-start(bf16[2,128,128]{2,1,0:T(8,128)(2,1)S(1)} %get-tuple-element.131), channel_id=1, source_target_pairs={{0,5},{1,4},{2,7},{3,6},{4,1},{5,0},{6,3},{7,2},{8,13},{9,12},{10,... | collective-permute-start | bytes 196616 | tf_op jit(solution)/shard_map/ppermute | solution.py:53
  46.6 8.8 %collective-permute-start.12 = (bf16[2,128,128]{2,1,0:T(8,128)(2,1)S(1)}, bf16[2,128,128]{2,1,0:T(8,128)(2,1)S(1)}, u32[]{:S(2)}, u32[]{:S(2)}) collective-permute-start(bf16[2,128,128]{2,1,0:T(8,128)(2,1)S(1)} %get-tuple-element.129), channel_id=1, source_target_pairs={{0,1},{1,0},{2,3},{3,2},{4,5},{5,4},{6,7},{7,6},{8,9},{9,8},{10,11... | collective-permute-start | bytes 196616 | tf_op jit(solution)/shard_map/ppermute | solution.py:53
  55.5 7.1 %collective-permute-start.17 = (bf16[2,128,128]{2,1,0:T(8,128)(2,1)S(1)}, bf16[2,128,128]{2,1,0:T(8,128)(2,1)S(1)}, u32[]{:S(2)}, u32[]{:S(2)}) collective-permute-start(bf16[2,128,128]{2,1,0:T(8,128)(2,1)S(1)} %shard_map.88), channel_id=1, source_target_pairs={{0,8},{1,9},{2,10},{3,11},{4,12},{5,13},{6,14},{7,15},{8,0},{9,1},... | collective-permute-start | bytes 196616 | tf_op jit(solution)/shard_map/ppermute | solution.py:53
  55.5 7.1 %collective-permute-start.16 = (bf16[2,128,128]{2,1,0:T(8,128)(2,1)S(1)}, bf16[2,128,128]{2,1,0:T(8,128)(2,1)S(1)}, u32[]{:S(2)}, u32[]{:S(2)}) collective-permute-start(bf16[2,128,128]{2,1,0:T(8,128)(2,1)S(1)} %shard_map.88), channel_id=1, source_target_pairs={{0,16},{1,17},{2,18},{3,19},{4,20},{5,21},{6,22},{7,23},{8,24},{9,... | collective-permute-start | bytes 196616 | tf_op jit(solution)/shard_map/ppermute | solution.py:53
  57.3 6.1 %collective-permute-start.15 = (bf16[2,128,128]{2,1,0:T(8,128)(2,1)S(1)}, bf16[2,128,128]{2,1,0:T(8,128)(2,1)S(1)}, u32[]{:S(2)}, u32[]{:S(2)}) collective-permute-start(bf16[2,128,128]{2,1,0:T(8,128)(2,1)S(1)} %shard_map.88), channel_id=1, source_target_pairs={{0,24},{1,25},{2,26},{3,27},{4,28},{5,29},{6,30},{7,31},{8,16},{9,... | collective-permute-start | bytes 196616 | tf_op jit(solution)/shard_map/ppermute | solution.py:53
  63.4 9.3 %collective-permute-start.18 = (bf16[2,128,1024]{2,1,0:T(8,128)(2,1)S(1)}, bf16[2,128,1024]{2,1,0:T(8,128)(2,1)S(1)}, u32[]{:S(2)}, u32[]{:S(2)}) collective-permute-start(bf16[2,128,1024]{2,1,0:T(8,128)(2,1)S(1)} %get-tuple-element.170), channel_id=1, source_target_pairs={{0,2},{1,3},{2,0},{3,1},{4,6},{5,7},{6,4},{7,5},{8,10},{9,11},{10,... | collective-permute-start | bytes 1572872 | tf_op jit(solution)/shard_map/ppermute | solution.py:53
  63.5 5.8 %collective-permute-start.22 = (bf16[2,128,128]{2,1,0:T(8,128)(2,1)S(1)}, bf16[2,128,128]{2,1,0:T(8,128)(2,1)S(1)}, u32[]{:S(2)}, u32[]{:S(2)}) collective-permute-start(bf16[2,128,128]{2,1,0:T(8,128)(2,1)S(1)} %get-tuple-element.183), channel_id=1, source_target_pairs={{0,5},{1,4},{2,7},{3,6},{4,1},{5,0},{6,3},{7,2},{8,13},{9,12},{10,... | collective-permute-start | bytes 196616 | tf_op jit(solution)/shard_map/ppermute | solution.py:53
  64.7 5.6 %collective-permute-start.21 = (bf16[2,128,128]{2,1,0:T(8,128)(2,1)S(1)}, bf16[2,128,128]{2,1,0:T(8,128)(2,1)S(1)}, u32[]{:S(2)}, u32[]{:S(2)}) collective-permute-start(bf16[2,128,128]{2,1,0:T(8,128)(2,1)S(1)} %get-tuple-element.183), channel_id=1, source_target_pairs={{0,4},{1,5},{2,6},{3,7},{4,0},{5,1},{6,2},{7,3},{8,12},{9,13},{10,... | collective-permute-start | bytes 196616 | tf_op jit(solution)/shard_map/ppermute | solution.py:53
  65.7 5.8 %collective-permute-start.20 = (bf16[2,128,128]{2,1,0:T(8,128)(2,1)S(1)}, bf16[2,128,128]{2,1,0:T(8,128)(2,1)S(1)}, u32[]{:S(2)}, u32[]{:S(2)}) collective-permute-start(bf16[2,128,128]{2,1,0:T(8,128)(2,1)S(1)} %get-tuple-element.176.base), channel_id=1, source_target_pairs={{0,1},{1,0},{2,3},{3,2},{4,5},{5,4},{6,7},{7,6},{8,9},{9,8},{10,11... | collective-permute-start | bytes 196616 | tf_op jit(solution)/shard_map/ppermute | solution.py:53
  69.6 3.1 %collective-permute-start.24 = (bf16[2,128,256]{2,1,0:T(8,128)(2,1)S(1)}, bf16[2,128,256]{2,1,0:T(8,128)(2,1)S(1)}, u32[]{:S(2)}, u32[]{:S(2)}) collective-permute-start(bf16[2,128,256]{2,1,0:T(8,128)(2,1)S(1)} %get-tuple-element.187), channel_id=1, source_target_pairs={{0,2},{1,3},{2,0},{3,1},{4,6},{5,7},{6,4},{7,5},{8,10},{9,11},{10,... | collective-permute-start | bytes 393224 | tf_op jit(solution)/shard_map/ppermute | solution.py:53
  70.6 2.1 %collective-permute-start.25 = (bf16[2,128,256]{2,1,0:T(8,128)(2,1)S(1)}, bf16[2,128,256]{2,1,0:T(8,128)(2,1)S(1)}, u32[]{:S(2)}, u32[]{:S(2)}) collective-permute-start(bf16[2,128,256]{2,1,0:T(8,128)(2,1)S(1)} %get-tuple-element.188), channel_id=1, source_target_pairs={{0,2},{1,3},{2,0},{3,1},{4,6},{5,7},{6,4},{7,5},{8,10},{9,11},{10,... | collective-permute-start | bytes 393224 | tf_op jit(solution)/shard_map/ppermute | solution.py:53
  70.9 1.8 %collective-permute-start.23 = (bf16[2,128,256]{2,1,0:T(8,128)(2,1)S(1)}, bf16[2,128,256]{2,1,0:T(8,128)(2,1)S(1)}, u32[]{:S(2)}, u32[]{:S(2)}) collective-permute-start(bf16[2,128,256]{2,1,0:T(8,128)(2,1)S(1)} %get-tuple-element.186), channel_id=1, source_target_pairs={{0,2},{1,3},{2,0},{3,1},{4,6},{5,7},{6,4},{7,5},{8,10},{9,11},{10,... | collective-permute-start | bytes 393224 | tf_op jit(solution)/shard_map/ppermute | solution.py:53
  71.7 2.2 %collective-permute-start.26 = (bf16[2,128,256]{2,1,0:T(8,128)(2,1)S(1)}, bf16[2,128,256]{2,1,0:T(8,128)(2,1)S(1)}, u32[]{:S(2)}, u32[]{:S(2)}) collective-permute-start(bf16[2,128,256]{2,1,0:T(8,128)(2,1)S(1)} %get-tuple-element.193), channel_id=1, source_target_pairs={{0,2},{1,3},{2,0},{3,1},{4,6},{5,7},{6,4},{7,5},{8,10},{9,11},{10,... | collective-permute-start | bytes 393224 | tf_op jit(solution)/shard_map/ppermute | solution.py:53

commit v2 on v1

--- a/solution.py
+++ b/solution.py
@@ -13,7 +13,9 @@
 PLANE = 8
 GROUP = 4
 OWNERS = 4
-ARRIVAL = (0, 3, 2, 1)
+OUT = (3, 1, 2)
+BACK = (0, 3, 1, 2)
+ARRIVAL = (0, 3, 1, 2)
 
 eps = 1e-06
 
@@ -200,41 +202,46 @@
                 out[r, n, j] = total
 
 
-def within_kernel(heads, qg_own, qg_other, kv_own, kv_other, weights, attn):
-    causal = causal_mask(qg_own.shape[1])
-    for n, (qg, kv) in enumerate(((qg_own, kv_own), (qg_other, kv_other))):
-        for h in range(heads):
-            at = slice(h * DH, (h + 1) * DH)
-            w = jnp.where(causal, dot(qg[0, :, at], kv[0, :, at], (1, 1)), 0.0).astype(BF16)
-            weights[n, h] = w
-            attn[n, :, at] = dot(w, kv[1, :, at], (1, 0))
-
-
-def forward_kernel(share, r, qg_own, qg_other, within, base, local, grad_sum, att_own, att_other, d_attn, states, every):
-    for j in range(share):
-        _, at = share_columns(r, j, share)
-        to = slice(j * DH, (j + 1) * DH)
-        before = base[j].astype(F32)
-        total = 0.0
-        for n, (qg, out) in enumerate(((qg_own, att_own), (qg_other, att_other))):
-            state = (before + local[r, n, j]).astype(BF16)
-            states[n, j] = state
-            query = qg[0, :, at]
-            attn = within[n, :, at] + dot(query, state, (1, 0))
-            inverse = 1.0 / jnp.sqrt(jnp.mean(attn * attn, axis=1, keepdims=True) + eps)
-            normed = attn * inverse
-            out[:, to] = normed.astype(BF16)
-            cotangent = qg[1, :, at].astype(F32)
-            inner = jnp.mean(cotangent * normed, axis=1, keepdims=True)
-            d = ((cotangent - normed * inner) * inverse).astype(BF16)
-            d_attn[n, :, to] = d
-            grad = dot(query, d, (0, 0))
-            every[n, j] = grad.astype(BF16)
-            total = total + grad
-        grad_sum[j] = total.astype(BF16)
-
-
-def middle_kernel(share, qg_own, qg_other, kv_own, kv_other, weights, *refs):
+def within_kernel(heads, qg, kv, weights, attn):
+    causal = causal_mask(qg.shape[1])
+    for h in range(heads):
+        at = slice(h * DH, (h + 1) * DH)
+        w = jnp.where(causal, dot(qg[0, :, at], kv[0, :, at], (1, 1)), 0.0).astype(BF16)
+        weights[h] = w
+        attn[:, at] = dot(w, kv[1, :, at], (1, 0))
+
+
+def forward_kernel(
+    share, r, qg_own, qg_other, within_own, within_other, base, local, grad_sum, att_own, att_other, d_attn, states, every
+):
+    source, within, target = (qg_own, qg_other), (within_own, within_other), (att_own, att_other)
+
+    def mean(x):
+        return jnp.mean(x, axis=1, keepdims=True)
+
+    for group in [[(j, n) for j in range(share) for n in range(2)]]:
+        at = {j: share_columns(r, j, share)[1] for j, _ in group}
+        to = {j: slice(j * DH, (j + 1) * DH) for j, _ in group}
+        state = {(j, n): (base[j].astype(F32) + local[r, n, j]).astype(BF16) for j, n in group}
+        query = {(j, n): source[n][0, :, at[j]] for j, n in group}
+        attn = {(j, n): within[n][:, at[j]] + dot(query[j, n], state[j, n], (1, 0)) for j, n in group}
+        inverse = {i: lax.rsqrt(mean(attn[i] * attn[i]) + eps) for i in group}
+        normed = {i: attn[i] * inverse[i] for i in group}
+        cotangent = {(j, n): source[n][1, :, at[j]].astype(F32) for j, n in group}
+        inner = {i: mean(cotangent[i] * normed[i]) for i in group}
+        d = {i: ((cotangent[i] - normed[i] * inner[i]) * inverse[i]).astype(BF16) for i in group}
+        grad = {i: dot(query[i], d[i], (0, 0)) for i in group}
+        for j, n in group:
+            states[n, j] = state[j, n]
+            target[n][:, to[j]] = normed[j, n].astype(BF16)
+            d_attn[n, :, to[j]] = d[j, n]
+            every[n, j] = grad[j, n].astype(BF16)
+            if n == 1:
+                grad_sum[j] = (grad[j, 0] + grad[j, 1]).astype(BF16)
+
+
+def middle_kernel(share, qg_own, qg_other, kv_own, kv_other, weights_own, weights_other, *refs):
+    weights = weights_own, weights_other
     d_attn, states, att_other = refs[:OWNERS], refs[OWNERS : 2 * OWNERS], refs[2 * OWNERS : 3 * OWNERS]
     dq_own, send, key_part, value_part = refs[3 * OWNERS :]
     causal = causal_mask(qg_own.shape[1])
@@ -252,7 +259,7 @@
                 else:
                     send[1, :, at] = d_query
                 key_part[n, :, at] = dot(dw, qg[0, :, at], (0, 0))
-                value_part[n, :, at] = dot(weights[n, head], d, (0, 0))
+                value_part[n, :, at] = dot(weights[n][head], d, (0, 0))
 
 
 def final_kernel(share, r, kv_own, kv_other, key_part, value_part, base, local, own, send):
@@ -279,12 +286,12 @@
     count = lax.axis_size(AXES[0]) * lax.axis_size(AXES[1])
     _, near, _ = pair_bit()
     received = [sums[0]] + [None] * (OWNERS - 1)
-    for r in (3, 2, 1):
+    for r in OUT:
         received[r] = swap(sums[r], owner_xor(r))
     direct = swap(every, near)
     shape = jax.ShapeDtypeStruct(sums[0].shape, BF16)
     (total,) = call(sum_kernel, received, [shape], grant=4)
-    total, later = lax.optimization_barrier((total, later))
+    total, later = lax.optimization_barrier((total, later)) if reverse else (total, later)
     others, steps = [], []
     levels = radices(count // PLANE)
     for level, masks in enumerate(levels):
@@ -297,7 +304,7 @@
     mine, across = call(functools.partial(base_kernel, reverse, steps), [*received, *others], [shape] * 2, grant=4)
     (local,) = call(functools.partial(local_kernel, reverse), [every, direct], [jax.ShapeDtypeStruct(every.shape, F32)])
     bases = [mine] + [None] * (OWNERS - 1)
-    for r in (3, 2, 1):
+    for r in ARRIVAL[1:]:
         bases[r] = swap(across if r & 2 else mine, owner_xor(r))
     return bases, local, done
 
@@ -348,16 +355,24 @@
     qg_other = swap(qg_send, pair)
 
     def within_work(*operands):
-        return call(
-            functools.partial(within_kernel, heads), operands, [of((2, heads, rows, rows), BF16), wide], 2 * one
-        )
-
-    bases, local, (weights, within) = scan(sums, every, False, within_work, (qg_own, qg_other, kv_own, kv_other))
+        found = []
+        for n in range(2):
+            found += call(
+                functools.partial(within_kernel, heads),
+                operands[2 * n : 2 * n + 2],
+                [of((heads, rows, rows), BF16), of((rows, half), F32)],
+                one,
+            )
+        return found
+
+    bases, local, (weights_own, within_own, weights_other, within_other) = scan(
+        sums, every, False, within_work, (qg_own, kv_own, qg_other, kv_other)
+    )
     results = [None] * OWNERS
-    for r in ARRIVAL:
+    for r in BACK:
         results[r] = call(
             functools.partial(forward_kernel, share, r),
-            [qg_own, qg_other, within, bases[r], local],
+            [qg_own, qg_other, within_own, within_other, bases[r], local],
             [state, part, part, part_two, state_two, state_two],
             2 * one // OWNERS,
         )
@@ -368,22 +383,30 @@
         return call(functools.partial(middle_kernel, share), operands, [flat, flat_two, wide, wide], 5 * one)
 
     bases, local, (dq_own, send, key_part, value_part) = scan(
-        grad_sums, every, True, middle_work, (qg_own, qg_other, kv_own, kv_other, weights, *d_attn, *states, *att_other)
+        grad_sums,
+        every,
+        True,
+        middle_work,
+        (qg_own, qg_other, kv_own, kv_other, weights_own, weights_other, *d_attn, *states, *att_other),
     )
     swapped = swap(send, pair)
     attended, grad_queries = call(
         join_own_kernel, [*att_own, dq_own], [full] * 2, hbm_out=True, scratch=[sems((OWNERS + 1,))]
     )
-    own, received = [None] * OWNERS, [None] * OWNERS
+    own, received, send = [None] * OWNERS, [None] * OWNERS, None
     for r in ARRIVAL:
+        if send is not None:
+            bases[r], send = lax.optimization_barrier((bases[r], send))
+            received[last] = swap(send, pair)
+        last = r
         own[r], send = call(
             functools.partial(final_kernel, share, r),
             [kv_own, kv_other, key_part, value_part, bases[r], local],
             [part_two] * 2,
             2 * one // OWNERS,
         )
-        received[r] = swap(send, pair)
-    early = OWNERS - 1
+    received[last] = swap(send, pair)
+    early = 1
     attended, grad_queries, grad_keys, grad_values = call(
         functools.partial(join_most_kernel, early),
         [attended, grad_queries, swapped, *own, *(received[r] for r in ARRIVAL[:early])],

time: 74.9 us -> 74.4 us (level)
  waiting for transfers between devices: 30.2 us -> 29.4 us
    ppermute x27, waiting for transfers between devices: 30.2 us -> 29.4 us  [swap(): return lax.ppermute(x, AXES, [(i, i ^ bits) for i in range(count)])]
    pallas_call x25 -> x26, Pallas kernels: 15 us -> 14.9 us  [call(): pl.pallas_call(kernel, out_shape=list(outs), in_specs=[pl.BlockSpec(memor...]
  transfers between devices with their start and end apart: 27 -> 27, of which waited for: 13 -> 12; matrix products, arithmetic and copies ran while one was open for 0% -> 0% of each run, Pallas kernels for 16% -> 16%
where the time goes in v2:
time: 74.4 us; the launch traced here: 74.2 us
  waiting for transfers between devices  29.4 us (40%)
  starting transfers between devices  28.6 us (38%)
  Pallas kernels  14.9 us (20%)
  between operations  0.93 us (1%)
    ppermute x27, waiting for transfers between devices, swap(): return lax.ppermute(x, AXES, [(i, i ^ bits) for i in range(count)])  29.4 us
    ppermute x27, starting transfers between devices, swap(): return lax.ppermute(x, AXES, [(i, i ^ bits) for i in range(count)])  28.6 us
    pallas_call x26, Pallas kernels, call(): pl.pallas_call(kernel, out_shape=list(outs), in_specs=[pl.BlockSpec(memor...  14.9 us
  transfers between devices with their start and end apart: 27, of which 12 were waited for; matrix products, arithmetic and copies ran while one was open for 0% of the time, Pallas kernels for 16%

profile of v2, /device:TPU:0, one launch (start us, length us, event | category | flops | bytes accessed | tf_op | source)
XLA Modules:
  0.0 74.2 jit_solution(4689736482426076042)
XLA Ops:
  0.6 1.1 %shard_map.76 = bf16[2,128,1024]{2,1,0:T(8,128)(2,1)S(1)} custom-call(bf16[128,2048]{1,0:T(8,128)(2,1)} %a.3, bf16[128,2048]{1,0:T(8,128)(2,1)} %b.3), custom_call_target="tpu_custom_call" | custom-call | bytes 1572864 | tf_op jit(solution)/shard_map/pallas_call | solution.py:62
  1.8 0.6 collective-permute-start
  2.3 1.1 %shard_map.75.own.kv.kv_own = bf16[2,128,1024]{2,1,0:T(8,128)(2,1)S(1)} custom-call(bf16[128,2048]{1,0:T(8,128)(2,1)} %a.3, bf16[128,2048]{1,0:T(8,128)(2,1)} %b.3), custom_call_target="tpu_custom_call" | custom-call | bytes 1572864 | tf_op jit(solution)/shard_map/pallas_call | solution.py:62
  3.5 0.4 collective-permute-done.other.kv.kv_other
  3.9 0.5 shard_map.77
  4.9 2.9 %collective-permute-start.8 = (bf16[4,2,2,128,128]{4,3,2,1,0:T(8,128)(2,1)S(1)}, bf16[4,2,2,128,128]{4,3,2,1,0:T(8,128)(2,1)S(1)}, u32[]{:S(2)}, u32[]{:S(2)}) collective-permute-start(bf16[4,2,2,128,128]{4,3,2,1,0:T(8,128)(2,1)S(1)} %get-tuple-element.126.every), channel_id=1, source_target_pairs={{0,1},{1,0},{2,3},{3,2},{4,5},{5,4},{6,7},{7,6},{8,9},{9,8},{10,11... | collective-permute-start | bytes 1572872 | tf_op jit(solution)/shard_map/ppermute | solution.py:55
  7.8 2.0 %collective-permute-start.3 = (bf16[2,128,128]{2,1,0:T(8,128)(2,1)S(1)}, bf16[2,128,128]{2,1,0:T(8,128)(2,1)S(1)}, u32[]{:S(2)}, u32[]{:S(2)}) collective-permute-start(bf16[2,128,128]{2,1,0:T(8,128)(2,1)S(1)} %get-tuple-element.114), channel_id=1, source_target_pairs={{0,4},{1,5},{2,6},{3,7},{4,0},{5,1},{6,2},{7,3},{8,12},{9,13},{10,... | collective-permute-start | bytes 196616 | tf_op jit(solution)/shard_map/ppermute | solution.py:55
  9.9 1.4 %collective-permute-start.4 = (bf16[2,128,128]{2,1,0:T(8,128)(2,1)S(1)}, bf16[2,128,128]{2,1,0:T(8,128)(2,1)S(1)}, u32[]{:S(2)}, u32[]{:S(2)}) collective-permute-start(bf16[2,128,128]{2,1,0:T(8,128)(2,1)S(1)} %get-tuple-element.115), channel_id=1, source_target_pairs={{0,5},{1,4},{2,7},{3,6},{4,1},{5,0},{6,3},{7,2},{8,13},{9,12},{10,... | collective-permute-start | bytes 196616 | tf_op jit(solution)/shard_map/ppermute | solution.py:55
  11.3 10.7 %collective-permute-done.2.refs_1_ = bf16[2,128,128]{2,1,0:T(8,128)(2,1)S(1)} collective-permute-done((bf16[2,128,128]{2,1,0:T(8,128)(2,1)S(1)}, bf16[2,128,128]{2,1,0:T(8,128)(2,1)S(1)}, u32[]{:S(2)}, u32[]{:S(2)}) %collective-permute-start.2) | collective-permute-done | bytes 65568 | tf_op jit(solution)/shard_map/ppermute | solution.py:55
  22.0 2.0 %collective-permute-done.4.refs_3_ = bf16[2,128,128]{2,1,0:T(8,128)(2,1)S(1)} collective-permute-done((bf16[2,128,128]{2,1,0:T(8,128)(2,1)S(1)}, bf16[2,128,128]{2,1,0:T(8,128)(2,1)S(1)}, u32[]{:S(2)}, u32[]{:S(2)}) %collective-permute-start.4) | collective-permute-done | bytes 65568 | tf_op jit(solution)/shard_map/ppermute | solution.py:55
  24.0 1.6 %collective-permute-start.7 = (bf16[2,128,128]{2,1,0:T(8,128)(2,1)S(1)}, bf16[2,128,128]{2,1,0:T(8,128)(2,1)S(1)}, u32[]{:S(2)}, u32[]{:S(2)}) collective-permute-start(bf16[2,128,128]{2,1,0:T(8,128)(2,1)S(1)} %shard_map.80), channel_id=1, source_target_pairs={{0,8},{1,9},{2,10},{3,11},{4,12},{5,13},{6,14},{7,15},{8,0},{9,1},... | collective-permute-start | bytes 196616 | tf_op jit(solution)/shard_map/ppermute | solution.py:55
  25.7 2.6 %collective-permute-start.6 = (bf16[2,128,128]{2,1,0:T(8,128)(2,1)S(1)}, bf16[2,128,128]{2,1,0:T(8,128)(2,1)S(1)}, u32[]{:S(2)}, u32[]{:S(2)}) collective-permute-start(bf16[2,128,128]{2,1,0:T(8,128)(2,1)S(1)} %shard_map.80), channel_id=1, source_target_pairs={{0,16},{1,17},{2,18},{3,19},{4,20},{5,21},{6,22},{7,23},{8,24},{9,... | collective-permute-start | bytes 196616 | tf_op jit(solution)/shard_map/ppermute | solution.py:55
  28.5 1.3 %shard_map.81 = (bf16[8,128,128]{2,1,0:T(8,128)(2,1)S(1)}, f32[128,1024]{1,0:T(8,128)S(1)}) custom-call(bf16[2,128,1024]{2,1,0:T(8,128)(2,1)S(1)} %shard_map.78.qg.qg_own, bf16[2,128,1024]{2,1,0:T(8,128)(2,1)S(1)} %shard_map.75.own.kv.kv_own), custom_call_target="tpu_custom_call" | custom-call | flops 67108864 | bytes 1835008 | tf_op jit(solution)/shard_map/pallas_call | solution.py:62
  29.9 1.3 %shard_map.82 = (bf16[8,128,128]{2,1,0:T(8,128)(2,1)S(1)}, f32[128,1024]{1,0:T(8,128)S(1)}) custom-call(bf16[2,128,1024]{2,1,0:T(8,128)(2,1)S(1)} %collective-permute-done.1.qg.qg_other, bf16[2,128,1024]{2,1,0:T(8,128)(2,1)S(1)} %collective-permute-done.other.kv.kv_other), custom_call_target="tpu_custom_call" | custom-call | flops 67108864 | bytes 1835008 | tf_op jit(solution)/shard_map/pallas_call | solution.py:62
  31.3 1.0 %collective-permute-done.6.refs_5_ = bf16[2,128,128]{2,1,0:T(8,128)(2,1)S(1)} collective-permute-done((bf16[2,128,128]{2,1,0:T(8,128)(2,1)S(1)}, bf16[2,128,128]{2,1,0:T(8,128)(2,1)S(1)}, u32[]{:S(2)}, u32[]{:S(2)}) %collective-permute-start.6) | collective-permute-done | bytes 65568 | tf_op jit(solution)/shard_map/ppermute | solution.py:55
  32.2 2.1 %collective-permute-done.5.refs_4_ = bf16[2,128,128]{2,1,0:T(8,128)(2,1)S(1)} collective-permute-done((bf16[2,128,128]{2,1,0:T(8,128)(2,1)S(1)}, bf16[2,128,128]{2,1,0:T(8,128)(2,1)S(1)}, u32[]{:S(2)}, u32[]{:S(2)}) %collective-permute-start.5) | collective-permute-done | bytes 65568 | tf_op jit(solution)/shard_map/ppermute | solution.py:55
  34.4 0.6 collective-permute-start.10
  35.0 2.4 %collective-permute-start.11 = (bf16[2,128,128]{2,1,0:T(8,128)(2,1)S(1)}, bf16[2,128,128]{2,1,0:T(8,128)(2,1)S(1)}, u32[]{:S(2)}, u32[]{:S(2)}) collective-permute-start(bf16[2,128,128]{2,1,0:T(8,128)(2,1)S(1)} %get-tuple-element.129), channel_id=1, source_target_pairs={{0,5},{1,4},{2,7},{3,6},{4,1},{5,0},{6,3},{7,2},{8,13},{9,12},{10,... | collective-permute-start | bytes 196616 | tf_op jit(solution)/shard_map/ppermute | solution.py:55
  37.4 0.5 collective-permute-start.9
  38.0 0.3 shard_map.84.local
  38.2 0.5 shard_map.85
  38.8 0.5 shard_map.87
  39.3 0.8 %collective-permute-done.11.base = bf16[2,128,128]{2,1,0:T(8,128)(2,1)S(1)} collective-permute-done((bf16[2,128,128]{2,1,0:T(8,128)(2,1)S(1)}, bf16[2,128,128]{2,1,0:T(8,128)(2,1)S(1)}, u32[]{:S(2)}, u32[]{:S(2)}) %collective-permute-start.11) | collective-permute-done | bytes 65568 | tf_op jit(solution)/shard_map/ppermute | solution.py:55
  40.1 0.5 shard_map.88
  40.7 1.7 %collective-permute-done.9.base = bf16[2,128,128]{2,1,0:T(8,128)(2,1)S(1)} collective-permute-done((bf16[2,128,128]{2,1,0:T(8,128)(2,1)S(1)}, bf16[2,128,128]{2,1,0:T(8,128)(2,1)S(1)}, u32[]{:S(2)}, u32[]{:S(2)}) %collective-permute-start.9) | collective-permute-done | bytes 65568 | tf_op jit(solution)/shard_map/ppermute | solution.py:55
  42.4 0.5 shard_map.86
  43.0 0.9 %collective-permute-start.19 = (bf16[4,2,2,128,128]{4,3,2,1,0:T(8,128)(2,1)S(1)}, bf16[4,2,2,128,128]{4,3,2,1,0:T(8,128)(2,1)S(1)}, u32[]{:S(2)}, u32[]{:S(2)}) collective-permute-start(bf16[4,2,2,128,128]{4,3,2,1,0:T(8,128)(2,1)S(1)} %shard_map.93.every), channel_id=1, source_target_pairs={{0,1},{1,0},{2,3},{3,2},{4,5},{5,4},{6,7},{7,6},{8,9},{9,8},{10,11... | collective-permute-start | bytes 1572872 | tf_op jit(solution)/shard_map/ppermute | solution.py:55
  43.8 0.6 collective-permute-start.13
  44.4 2.1 %collective-permute-start.14 = (bf16[2,128,128]{2,1,0:T(8,128)(2,1)S(1)}, bf16[2,128,128]{2,1,0:T(8,128)(2,1)S(1)}, u32[]{:S(2)}, u32[]{:S(2)}) collective-permute-start(bf16[2,128,128]{2,1,0:T(8,128)(2,1)S(1)} %get-tuple-element.135), channel_id=1, source_target_pairs={{0,5},{1,4},{2,7},{3,6},{4,1},{5,0},{6,3},{7,2},{8,13},{9,12},{10,... | collective-permute-start | bytes 196616 | tf_op jit(solution)/shard_map/ppermute | solution.py:55
  46.5 0.8 %collective-permute-start.12 = (bf16[2,128,128]{2,1,0:T(8,128)(2,1)S(1)}, bf16[2,128,128]{2,1,0:T(8,128)(2,1)S(1)}, u32[]{:S(2)}, u32[]{:S(2)}) collective-permute-start(bf16[2,128,128]{2,1,0:T(8,128)(2,1)S(1)} %get-tuple-element.133), channel_id=1, source_target_pairs={{0,1},{1,0},{2,3},{3,2},{4,5},{5,4},{6,7},{7,6},{8,9},{9,8},{10,11... | collective-permute-start | bytes 196616 | tf_op jit(solution)/shard_map/ppermute | solution.py:55
  47.3 1.1 %collective-permute-done.13.refs_2_ = bf16[2,128,128]{2,1,0:T(8,128)(2,1)S(1)} collective-permute-done((bf16[2,128,128]{2,1,0:T(8,128)(2,1)S(1)}, bf16[2,128,128]{2,1,0:T(8,128)(2,1)S(1)}, u32[]{:S(2)}, u32[]{:S(2)}) %collective-permute-start.13) | collective-permute-done | bytes 65568 | tf_op jit(solution)/shard_map/ppermute | solution.py:55
  48.4 6.5 %collective-permute-done.14.refs_3_ = bf16[2,128,128]{2,1,0:T(8,128)(2,1)S(1)} collective-permute-done((bf16[2,128,128]{2,1,0:T(8,128)(2,1)S(1)}, bf16[2,128,128]{2,1,0:T(8,128)(2,1)S(1)}, u32[]{:S(2)}, u32[]{:S(2)}) %collective-permute-start.14) | collective-permute-done | bytes 65568 | tf_op jit(solution)/shard_map/ppermute | solution.py:55
  54.9 0.5 collective-permute-done.12.refs_1_
  55.5 1.9 %collective-permute-start.16 = (bf16[2,128,128]{2,1,0:T(8,128)(2,1)S(1)}, bf16[2,128,128]{2,1,0:T(8,128)(2,1)S(1)}, u32[]{:S(2)}, u32[]{:S(2)}) collective-permute-start(bf16[2,128,128]{2,1,0:T(8,128)(2,1)S(1)} %shard_map.89), channel_id=1, source_target_pairs={{0,16},{1,17},{2,18},{3,19},{4,20},{5,21},{6,22},{7,23},{8,24},{9,... | collective-permute-start | bytes 196616 | tf_op jit(solution)/shard_map/ppermute | solution.py:55
  57.3 2.5 %collective-permute-start.15 = (bf16[2,128,128]{2,1,0:T(8,128)(2,1)S(1)}, bf16[2,128,128]{2,1,0:T(8,128)(2,1)S(1)}, u32[]{:S(2)}, u32[]{:S(2)}) collective-permute-start(bf16[2,128,128]{2,1,0:T(8,128)(2,1)S(1)} %shard_map.89), channel_id=1, source_target_pairs={{0,24},{1,25},{2,26},{3,27},{4,28},{5,29},{6,30},{7,31},{8,16},{9,... | collective-permute-start | bytes 196616 | tf_op jit(solution)/shard_map/ppermute | solution.py:55
  59.9 2.7 %shard_map.90 = (bf16[128,1024]{1,0:T(8,128)(2,1)S(1)}, bf16[2,128,1024]{2,1,0:T(8,128)(2,1)S(1)}, f32[2,128,1024]{2,1,0:T(8,128)S(1)}, f32[2,128,1024]{2,1,0:T(8,128)S(1)}) custom-call(bf16[2,128,1024]{2,1,0:T(8,128)(2,1)S(1)} %shard_map.78.qg.qg_own, bf16[2,128,1024]{2,1,0:T(8,128)(2,1)S(1)} %collective-permute-done.1.qg.qg_other, ...), custom_call_target="tpu_custom_call" | custom-call | flops 335544320 | bytes 6815744 | tf_op jit(solution)/shard_map/pallas_call | solution.py:62
  62.6 0.8 %collective-permute-done.15.refs_4_ = bf16[2,128,128]{2,1,0:T(8,128)(2,1)S(1)} collective-permute-done((bf16[2,128,128]{2,1,0:T(8,128)(2,1)S(1)}, bf16[2,128,128]{2,1,0:T(8,128)(2,1)S(1)}, u32[]{:S(2)}, u32[]{:S(2)}) %collective-permute-start.15) | collective-permute-done | bytes 65568 | tf_op jit(solution)/shard_map/ppermute | solution.py:55
  63.5 1.1 %collective-permute-start.21 = (bf16[2,128,128]{2,1,0:T(8,128)(2,1)S(1)}, bf16[2,128,128]{2,1,0:T(8,128)(2,1)S(1)}, u32[]{:S(2)}, u32[]{:S(2)}) collective-permute-start(bf16[2,128,128]{2,1,0:T(8,128)(2,1)S(1)} %get-tuple-element.188), channel_id=1, source_target_pairs={{0,5},{1,4},{2,7},{3,6},{4,1},{5,0},{6,3},{7,2},{8,13},{9,12},{10,... | collective-permute-start | bytes 196616 | tf_op jit(solution)/shard_map/ppermute | solution.py:55
  64.6 1.2 %collective-permute-start.20 = (bf16[2,128,128]{2,1,0:T(8,128)(2,1)S(1)}, bf16[2,128,128]{2,1,0:T(8,128)(2,1)S(1)}, u32[]{:S(2)}, u32[]{:S(2)}) collective-permute-start(bf16[2,128,128]{2,1,0:T(8,128)(2,1)S(1)} %get-tuple-element.182.base), channel_id=1, source_target_pairs={{0,1},{1,0},{2,3},{3,2},{4,5},{5,4},{6,7},{7,6},{8,9},{9,8},{10,11... | collective-permute-start | bytes 196616 | tf_op jit(solution)/shard_map/ppermute | solution.py:55
  65.8 1.3 %collective-permute-start.22 = (bf16[2,128,128]{2,1,0:T(8,128)(2,1)S(1)}, bf16[2,128,128]{2,1,0:T(8,128)(2,1)S(1)}, u32[]{:S(2)}, u32[]{:S(2)}) collective-permute-start(bf16[2,128,128]{2,1,0:T(8,128)(2,1)S(1)} %get-tuple-element.188), channel_id=1, source_target_pairs={{0,4},{1,5},{2,6},{3,7},{4,0},{5,1},{6,2},{7,3},{8,12},{9,13},{10,... | collective-permute-start | bytes 196616 | tf_op jit(solution)/shard_map/ppermute | solution.py:55
  67.0 0.3 shard_map.94.local
  67.6 1.8 %collective-permute-done.21.base = bf16[2,128,128]{2,1,0:T(8,128)(2,1)S(1)} collective-permute-done((bf16[2,128,128]{2,1,0:T(8,128)(2,1)S(1)}, bf16[2,128,128]{2,1,0:T(8,128)(2,1)S(1)}, u32[]{:S(2)}, u32[]{:S(2)}) %collective-permute-start.21) | collective-permute-done | bytes 65568 | tf_op jit(solution)/shard_map/ppermute | solution.py:55
  69.7 0.6 collective-permute-start.24
  70.5 0.3 shard_map.98
  70.9 0.5 collective-permute-start.25
  71.4 0.8 %shard_map.91 = (bf16[128,2048]{1,0:T(8,128)(2,1)}, bf16[128,2048]{1,0:T(8,128)(2,1)}) custom-call(bf16[128,256]{1,0:T(8,128)(2,1)S(1)} %get-tuple-element.127.refs_0_, bf16[128,256]{1,0:T(8,128)(2,1)S(1)} %get-tuple-element.128.refs_1_, bf16[128,256]{1,0:T(8,128)(2,1)S(1)} %get-tuple-element.130.refs_2_, bf16[128,256]{1,0:T(8,128)(2,1)S(1)} %get-tuple-element.131.refs_3_, ...), custom_call_target="tpu_custom_call" | custom-call | bytes 1572864 | tf_op jit(solution)/shard_map/pallas_call | solution.py:62
  72.2 1.1 %shard_map.99 = (bf16[128,2048]{1,0:T(8,128)(2,1)}, bf16[128,2048]{1,0:T(8,128)(2,1)}, bf16[128,2048]{1,0:T(8,128)(2,1)}, bf16[128,2048]{1,0:T(8,128)(2,1)}) custom-call(bf16[128,2048]{1,0:T(8,128)(2,1)} %get-tuple-element.174.refs_0_, bf16[128,2048]{1,0:T(8,128)(2,1)} %get-tuple-element.175.refs_1_, ...), custom_call_target="tpu_custom_call", output_to_operand_aliasing={{0}: (0, {}), {1}: (1, {})} | custom-call | bytes 4325376 | tf_op jit(solution)/shard_map/pallas_call | solution.py:62
  73.4 0.8 %shard_map.100 = (bf16[128,2048]{1,0:T(8,128)(2,1)}, bf16[128,2048]{1,0:T(8,128)(2,1)}) custom-call(bf16[128,2048]{1,0:T(8,128)(2,1)} %get-tuple-element.201.refs_0_, bf16[128,2048]{1,0:T(8,128)(2,1)} %get-tuple-element.202.refs_1_, bf16[2,128,256]{2,1,0:T(8,128)(2,1)S(1)} %collective-permute-done.24.refs_2_, ...), custom_call_target="tpu_custom_call", output_to_operand_aliasing={{0}: (0, {}), {1}: (1, {})} | custom-call | bytes 2490368 | tf_op jit(solution)/shard_map/pallas_call | solution.py:62
  (36 shorter events, 2.1 us)
Async XLA Ops:
  1.8 2.1 %collective-permute-start = (bf16[2,128,1024]{2,1,0:T(8,128)(2,1)S(1)}, bf16[2,128,1024]{2,1,0:T(8,128)(2,1)S(1)}, u32[]{:S(2)}, u32[]{:S(2)}) collective-permute-start(bf16[2,128,1024]{2,1,0:T(8,128)(2,1)S(1)} %shard_map.76), channel_id=1, source_target_pairs={{0,2},{1,3},{2,0},{3,1},{4,6},{5,7},{6,4},{7,5},{8,10},{9,11},{10,... | collective-permute-start | bytes 1572872 | tf_op jit(solution)/shard_map/ppermute | solution.py:55
  3.5 1.0 %copy-start = (bf16[128,2048]{1,0:T(8,128)(2,1)S(1)}, bf16[128,2048]{1,0:T(8,128)(2,1)}, u32[]{:S(2)}) copy-start(bf16[128,2048]{1,0:T(8,128)(2,1)} %a.5) | copy-start | bytes 1572868
  3.5 1.2 %copy-start.1 = (bf16[128,2048]{1,0:T(8,128)(2,1)S(1)}, bf16[128,2048]{1,0:T(8,128)(2,1)}, u32[]{:S(2)}) copy-start(bf16[128,2048]{1,0:T(8,128)(2,1)} %b.5) | copy-start | bytes 1572868
  4.7 25.2 %collective-permute-start.1 = (bf16[2,128,1024]{2,1,0:T(8,128)(2,1)S(1)}, bf16[2,128,1024]{2,1,0:T(8,128)(2,1)S(1)}, u32[]{:S(2)}, u32[]{:S(2)}) collective-permute-start(bf16[2,128,1024]{2,1,0:T(8,128)(2,1)S(1)} %shard_map.79), channel_id=1, source_target_pairs={{0,2},{1,3},{2,0},{3,1},{4,6},{5,7},{6,4},{7,5},{8,10},{9,11},{10,... | collective-permute-start | bytes 1572872 | tf_op jit(solution)/shard_map/ppermute | solution.py:55
  4.9 33.1 %collective-permute-start.8 = (bf16[4,2,2,128,128]{4,3,2,1,0:T(8,128)(2,1)S(1)}, bf16[4,2,2,128,128]{4,3,2,1,0:T(8,128)(2,1)S(1)}, u32[]{:S(2)}, u32[]{:S(2)}) collective-permute-start(bf16[4,2,2,128,128]{4,3,2,1,0:T(8,128)(2,1)S(1)} %get-tuple-element.126.every), channel_id=1, source_target_pairs={{0,1},{1,0},{2,3},{3,2},{4,5},{5,4},{6,7},{7,6},{8,9},{9,8},{10,11... | collective-permute-start | bytes 1572872 | tf_op jit(solution)/shard_map/ppermute | solution.py:55
  7.8 14.2 %collective-permute-start.2 = (bf16[2,128,128]{2,1,0:T(8,128)(2,1)S(1)}, bf16[2,128,128]{2,1,0:T(8,128)(2,1)S(1)}, u32[]{:S(2)}, u32[]{:S(2)}) collective-permute-start(bf16[2,128,128]{2,1,0:T(8,128)(2,1)S(1)} %get-tuple-element.113), channel_id=1, source_target_pairs={{0,1},{1,0},{2,3},{3,2},{4,5},{5,4},{6,7},{7,6},{8,9},{9,8},{10,11... | collective-permute-start | bytes 196616 | tf_op jit(solution)/shard_map/ppermute | solution.py:55
  7.8 14.2 %collective-permute-start.3 = (bf16[2,128,128]{2,1,0:T(8,128)(2,1)S(1)}, bf16[2,128,128]{2,1,0:T(8,128)(2,1)S(1)}, u32[]{:S(2)}, u32[]{:S(2)}) collective-permute-start(bf16[2,128,128]{2,1,0:T(8,128)(2,1)S(1)} %get-tuple-element.114), channel_id=1, source_target_pairs={{0,4},{1,5},{2,6},{3,7},{4,0},{5,1},{6,2},{7,3},{8,12},{9,13},{10,... | collective-permute-start | bytes 196616 | tf_op jit(solution)/shard_map/ppermute | solution.py:55
  9.9 14.1 %collective-permute-start.4 = (bf16[2,128,128]{2,1,0:T(8,128)(2,1)S(1)}, bf16[2,128,128]{2,1,0:T(8,128)(2,1)S(1)}, u32[]{:S(2)}, u32[]{:S(2)}) collective-permute-start(bf16[2,128,128]{2,1,0:T(8,128)(2,1)S(1)} %get-tuple-element.115), channel_id=1, source_target_pairs={{0,5},{1,4},{2,7},{3,6},{4,1},{5,0},{6,3},{7,2},{8,13},{9,12},{10,... | collective-permute-start | bytes 196616 | tf_op jit(solution)/shard_map/ppermute | solution.py:55
  24.0 7.2 %collective-permute-start.7 = (bf16[2,128,128]{2,1,0:T(8,128)(2,1)S(1)}, bf16[2,128,128]{2,1,0:T(8,128)(2,1)S(1)}, u32[]{:S(2)}, u32[]{:S(2)}) collective-permute-start(bf16[2,128,128]{2,1,0:T(8,128)(2,1)S(1)} %shard_map.80), channel_id=1, source_target_pairs={{0,8},{1,9},{2,10},{3,11},{4,12},{5,13},{6,14},{7,15},{8,0},{9,1},... | collective-permute-start | bytes 196616 | tf_op jit(solution)/shard_map/ppermute | solution.py:55
  25.7 6.6 %collective-permute-start.6 = (bf16[2,128,128]{2,1,0:T(8,128)(2,1)S(1)}, bf16[2,128,128]{2,1,0:T(8,128)(2,1)S(1)}, u32[]{:S(2)}, u32[]{:S(2)}) collective-permute-start(bf16[2,128,128]{2,1,0:T(8,128)(2,1)S(1)} %shard_map.80), channel_id=1, source_target_pairs={{0,16},{1,17},{2,18},{3,19},{4,20},{5,21},{6,22},{7,23},{8,24},{9,... | collective-permute-start | bytes 196616 | tf_op jit(solution)/shard_map/ppermute | solution.py:55
  28.3 6.1 %collective-permute-start.5 = (bf16[2,128,128]{2,1,0:T(8,128)(2,1)S(1)}, bf16[2,128,128]{2,1,0:T(8,128)(2,1)S(1)}, u32[]{:S(2)}, u32[]{:S(2)}) collective-permute-start(bf16[2,128,128]{2,1,0:T(8,128)(2,1)S(1)} %shard_map.80), channel_id=1, source_target_pairs={{0,24},{1,25},{2,26},{3,27},{4,28},{5,29},{6,30},{7,31},{8,16},{9,... | collective-permute-start | bytes 196616 | tf_op jit(solution)/shard_map/ppermute | solution.py:55
  34.4 4.4 %collective-permute-start.10 = (bf16[2,128,128]{2,1,0:T(8,128)(2,1)S(1)}, bf16[2,128,128]{2,1,0:T(8,128)(2,1)S(1)}, u32[]{:S(2)}, u32[]{:S(2)}) collective-permute-start(bf16[2,128,128]{2,1,0:T(8,128)(2,1)S(1)} %get-tuple-element.129), channel_id=1, source_target_pairs={{0,4},{1,5},{2,6},{3,7},{4,0},{5,1},{6,2},{7,3},{8,12},{9,13},{10,... | collective-permute-start | bytes 196616 | tf_op jit(solution)/shard_map/ppermute | solution.py:55
  35.0 5.2 %collective-permute-start.11 = (bf16[2,128,128]{2,1,0:T(8,128)(2,1)S(1)}, bf16[2,128,128]{2,1,0:T(8,128)(2,1)S(1)}, u32[]{:S(2)}, u32[]{:S(2)}) collective-permute-start(bf16[2,128,128]{2,1,0:T(8,128)(2,1)S(1)} %get-tuple-element.129), channel_id=1, source_target_pairs={{0,5},{1,4},{2,7},{3,6},{4,1},{5,0},{6,3},{7,2},{8,13},{9,12},{10,... | collective-permute-start | bytes 196616 | tf_op jit(solution)/shard_map/ppermute | solution.py:55
  37.4 5.0 %collective-permute-start.9 = (bf16[2,128,128]{2,1,0:T(8,128)(2,1)S(1)}, bf16[2,128,128]{2,1,0:T(8,128)(2,1)S(1)}, u32[]{:S(2)}, u32[]{:S(2)}) collective-permute-start(bf16[2,128,128]{2,1,0:T(8,128)(2,1)S(1)} %get-tuple-element.125.base), channel_id=1, source_target_pairs={{0,1},{1,0},{2,3},{3,2},{4,5},{5,4},{6,7},{7,6},{8,9},{9,8},{10,11... | collective-permute-start | bytes 196616 | tf_op jit(solution)/shard_map/ppermute | solution.py:55
  43.0 24.1 %collective-permute-start.19 = (bf16[4,2,2,128,128]{4,3,2,1,0:T(8,128)(2,1)S(1)}, bf16[4,2,2,128,128]{4,3,2,1,0:T(8,128)(2,1)S(1)}, u32[]{:S(2)}, u32[]{:S(2)}) collective-permute-start(bf16[4,2,2,128,128]{4,3,2,1,0:T(8,128)(2,1)S(1)} %shard_map.93.every), channel_id=1, source_target_pairs={{0,1},{1,0},{2,3},{3,2},{4,5},{5,4},{6,7},{7,6},{8,9},{9,8},{10,11... | collective-permute-start | bytes 1572872 | tf_op jit(solution)/shard_map/ppermute | solution.py:55
  43.8 4.6 %collective-permute-start.13 = (bf16[2,128,128]{2,1,0:T(8,128)(2,1)S(1)}, bf16[2,128,128]{2,1,0:T(8,128)(2,1)S(1)}, u32[]{:S(2)}, u32[]{:S(2)}) collective-permute-start(bf16[2,128,128]{2,1,0:T(8,128)(2,1)S(1)} %get-tuple-element.134), channel_id=1, source_target_pairs={{0,4},{1,5},{2,6},{3,7},{4,0},{5,1},{6,2},{7,3},{8,12},{9,13},{10,... | collective-permute-start | bytes 196616 | tf_op jit(solution)/shard_map/ppermute | solution.py:55
  44.4 10.4 %collective-permute-start.14 = (bf16[2,128,128]{2,1,0:T(8,128)(2,1)S(1)}, bf16[2,128,128]{2,1,0:T(8,128)(2,1)S(1)}, u32[]{:S(2)}, u32[]{:S(2)}) collective-permute-start(bf16[2,128,128]{2,1,0:T(8,128)(2,1)S(1)} %get-tuple-element.135), channel_id=1, source_target_pairs={{0,5},{1,4},{2,7},{3,6},{4,1},{5,0},{6,3},{7,2},{8,13},{9,12},{10,... | collective-permute-start | bytes 196616 | tf_op jit(solution)/shard_map/ppermute | solution.py:55
  46.5 8.8 %collective-permute-start.12 = (bf16[2,128,128]{2,1,0:T(8,128)(2,1)S(1)}, bf16[2,128,128]{2,1,0:T(8,128)(2,1)S(1)}, u32[]{:S(2)}, u32[]{:S(2)}) collective-permute-start(bf16[2,128,128]{2,1,0:T(8,128)(2,1)S(1)} %get-tuple-element.133), channel_id=1, source_target_pairs={{0,1},{1,0},{2,3},{3,2},{4,5},{5,4},{6,7},{7,6},{8,9},{9,8},{10,11... | collective-permute-start | bytes 196616 | tf_op jit(solution)/shard_map/ppermute | solution.py:55
  55.4 7.1 %collective-permute-start.17 = (bf16[2,128,128]{2,1,0:T(8,128)(2,1)S(1)}, bf16[2,128,128]{2,1,0:T(8,128)(2,1)S(1)}, u32[]{:S(2)}, u32[]{:S(2)}) collective-permute-start(bf16[2,128,128]{2,1,0:T(8,128)(2,1)S(1)} %shard_map.89), channel_id=1, source_target_pairs={{0,8},{1,9},{2,10},{3,11},{4,12},{5,13},{6,14},{7,15},{8,0},{9,1},... | collective-permute-start | bytes 196616 | tf_op jit(solution)/shard_map/ppermute | solution.py:55
  55.5 7.1 %collective-permute-start.16 = (bf16[2,128,128]{2,1,0:T(8,128)(2,1)S(1)}, bf16[2,128,128]{2,1,0:T(8,128)(2,1)S(1)}, u32[]{:S(2)}, u32[]{:S(2)}) collective-permute-start(bf16[2,128,128]{2,1,0:T(8,128)(2,1)S(1)} %shard_map.89), channel_id=1, source_target_pairs={{0,16},{1,17},{2,18},{3,19},{4,20},{5,21},{6,22},{7,23},{8,24},{9,... | collective-permute-start | bytes 196616 | tf_op jit(solution)/shard_map/ppermute | solution.py:55
  57.3 6.1 %collective-permute-start.15 = (bf16[2,128,128]{2,1,0:T(8,128)(2,1)S(1)}, bf16[2,128,128]{2,1,0:T(8,128)(2,1)S(1)}, u32[]{:S(2)}, u32[]{:S(2)}) collective-permute-start(bf16[2,128,128]{2,1,0:T(8,128)(2,1)S(1)} %shard_map.89), channel_id=1, source_target_pairs={{0,24},{1,25},{2,26},{3,27},{4,28},{5,29},{6,30},{7,31},{8,16},{9,... | collective-permute-start | bytes 196616 | tf_op jit(solution)/shard_map/ppermute | solution.py:55
  63.4 8.8 %collective-permute-start.18 = (bf16[2,128,1024]{2,1,0:T(8,128)(2,1)S(1)}, bf16[2,128,1024]{2,1,0:T(8,128)(2,1)S(1)}, u32[]{:S(2)}, u32[]{:S(2)}) collective-permute-start(bf16[2,128,1024]{2,1,0:T(8,128)(2,1)S(1)} %get-tuple-element.176), channel_id=1, source_target_pairs={{0,2},{1,3},{2,0},{3,1},{4,6},{5,7},{6,4},{7,5},{8,10},{9,11},{10,... | collective-permute-start | bytes 1572872 | tf_op jit(solution)/shard_map/ppermute | solution.py:55
  63.5 5.9 %collective-permute-start.21 = (bf16[2,128,128]{2,1,0:T(8,128)(2,1)S(1)}, bf16[2,128,128]{2,1,0:T(8,128)(2,1)S(1)}, u32[]{:S(2)}, u32[]{:S(2)}) collective-permute-start(bf16[2,128,128]{2,1,0:T(8,128)(2,1)S(1)} %get-tuple-element.188), channel_id=1, source_target_pairs={{0,5},{1,4},{2,7},{3,6},{4,1},{5,0},{6,3},{7,2},{8,13},{9,12},{10,... | collective-permute-start | bytes 196616 | tf_op jit(solution)/shard_map/ppermute | solution.py:55
  64.6 5.1 %collective-permute-start.20 = (bf16[2,128,128]{2,1,0:T(8,128)(2,1)S(1)}, bf16[2,128,128]{2,1,0:T(8,128)(2,1)S(1)}, u32[]{:S(2)}, u32[]{:S(2)}) collective-permute-start(bf16[2,128,128]{2,1,0:T(8,128)(2,1)S(1)} %get-tuple-element.182.base), channel_id=1, source_target_pairs={{0,1},{1,0},{2,3},{3,2},{4,5},{5,4},{6,7},{7,6},{8,9},{9,8},{10,11... | collective-permute-start | bytes 196616 | tf_op jit(solution)/shard_map/ppermute | solution.py:55
  65.8 4.7 %collective-permute-start.22 = (bf16[2,128,128]{2,1,0:T(8,128)(2,1)S(1)}, bf16[2,128,128]{2,1,0:T(8,128)(2,1)S(1)}, u32[]{:S(2)}, u32[]{:S(2)}) collective-permute-start(bf16[2,128,128]{2,1,0:T(8,128)(2,1)S(1)} %get-tuple-element.188), channel_id=1, source_target_pairs={{0,4},{1,5},{2,6},{3,7},{4,0},{5,1},{6,2},{7,3},{8,12},{9,13},{10,... | collective-permute-start | bytes 196616 | tf_op jit(solution)/shard_map/ppermute | solution.py:55
  69.4 2.8 %collective-permute-start.23 = (bf16[2,128,256]{2,1,0:T(8,128)(2,1)S(1)}, bf16[2,128,256]{2,1,0:T(8,128)(2,1)S(1)}, u32[]{:S(2)}, u32[]{:S(2)}) collective-permute-start(bf16[2,128,256]{2,1,0:T(8,128)(2,1)S(1)} %get-tuple-element.198), channel_id=1, source_target_pairs={{0,2},{1,3},{2,0},{3,1},{4,6},{5,7},{6,4},{7,5},{8,10},{9,11},{10,... | collective-permute-start | bytes 393224 | tf_op jit(solution)/shard_map/ppermute | solution.py:55
  69.7 3.7 %collective-permute-start.24 = (bf16[2,128,256]{2,1,0:T(8,128)(2,1)S(1)}, bf16[2,128,256]{2,1,0:T(8,128)(2,1)S(1)}, u32[]{:S(2)}, u32[]{:S(2)}) collective-permute-start(bf16[2,128,256]{2,1,0:T(8,128)(2,1)S(1)} %get-tuple-element.203), channel_id=1, source_target_pairs={{0,2},{1,3},{2,0},{3,1},{4,6},{5,7},{6,4},{7,5},{8,10},{9,11},{10,... | collective-permute-start | bytes 393224 | tf_op jit(solution)/shard_map/ppermute | solution.py:55
  70.8 2.6 %collective-permute-start.26 = (bf16[2,128,256]{2,1,0:T(8,128)(2,1)S(1)}, bf16[2,128,256]{2,1,0:T(8,128)(2,1)S(1)}, u32[]{:S(2)}, u32[]{:S(2)}) collective-permute-start(bf16[2,128,256]{2,1,0:T(8,128)(2,1)S(1)} %get-tuple-element.205), channel_id=1, source_target_pairs={{0,2},{1,3},{2,0},{3,1},{4,6},{5,7},{6,4},{7,5},{8,10},{9,11},{10,... | collective-permute-start | bytes 393224 | tf_op jit(solution)/shard_map/ppermute | solution.py:55
  70.9 2.5 %collective-permute-start.25 = (bf16[2,128,256]{2,1,0:T(8,128)(2,1)S(1)}, bf16[2,128,256]{2,1,0:T(8,128)(2,1)S(1)}, u32[]{:S(2)}, u32[]{:S(2)}) collective-permute-start(bf16[2,128,256]{2,1,0:T(8,128)(2,1)S(1)} %get-tuple-element.204), channel_id=1, source_target_pairs={{0,2},{1,3},{2,0},{3,1},{4,6},{5,7},{6,4},{7,5},{8,10},{9,11},{10,... | collective-permute-start | bytes 393224 | tf_op jit(solution)/shard_map/ppermute | solution.py:55

commit v3 on v2

--- a/solution.py
+++ b/solution.py
@@ -14,8 +14,9 @@
 GROUP = 4
 OWNERS = 4
 OUT = (3, 1, 2)
-BACK = (0, 3, 1, 2)
+BACK = (0, 1, 3, 2)
 ARRIVAL = (0, 3, 1, 2)
+TOGETHER = 3
 
 eps = 1e-06
 
@@ -136,11 +137,11 @@
     run_copies(copies)
 
 
-def join_rest_kernel(count, *refs):
-    received, outs, sems = refs[2 : 2 + OWNERS - count], refs[2 + OWNERS - count : -1], refs[-1]
+def join_rest_kernel(where, *refs):
+    received, outs, sems = refs[2:-3], refs[-3:-1], refs[-1]
     copies = []
-    for k, r in enumerate(ARRIVAL[count:]):
-        copies += [write_share(received[k].at[n], outs[n], True, r, sems.at[k, n]) for n in range(2)]
+    for r, (k, n) in enumerate(where):
+        copies += [write_share(received[k].at[n, m], outs[m], True, r, sems.at[r, m]) for m in range(2)]
     run_copies(copies)
 
 
@@ -262,7 +263,11 @@
                 value_part[n, :, at] = dot(weights[n][head], d, (0, 0))
 
 
-def final_kernel(share, r, kv_own, kv_other, key_part, value_part, base, local, own, send):
+def final_kernel(share, r, kv_own, kv_other, key_part, value_part, base, local, *refs):
+    earlier, (own, sends) = refs[:-2], refs[-2:]
+    for k, ref in enumerate(earlier):
+        sends[k] = ref[0]
+    send = sends.at[len(earlier)]
     for j in range(share):
         _, at = share_columns(r, j, share)
         to = slice(j * DH, (j + 1) * DH)
@@ -332,7 +337,7 @@
             [key_rows, value_rows],
             [flat_two],
             hbm_in=True,
-            scratch=[sems((2, 4))],
+            scratch=[sems((2, 1))],
             grant=53,
         )[0]
         for partner in (True, False)
@@ -393,34 +398,44 @@
     attended, grad_queries = call(
         join_own_kernel, [*att_own, dq_own], [full] * 2, hbm_out=True, scratch=[sems((OWNERS + 1,))]
     )
-    own, received, send = [None] * OWNERS, [None] * OWNERS, None
-    for r in ARRIVAL:
-        if send is not None:
-            bases[r], send = lax.optimization_barrier((bases[r], send))
-            received[last] = swap(send, pair)
-        last = r
+    own, received, waiting = [None] * OWNERS, [None] * OWNERS, []
+    for k, r in enumerate(ARRIVAL):
+        whole = k + 1 >= TOGETHER
+        earlier = waiting if whole else []
         own[r], send = call(
             functools.partial(final_kernel, share, r),
-            [kv_own, kv_other, key_part, value_part, bases[r], local],
-            [part_two] * 2,
+            [kv_own, kv_other, key_part, value_part, bases[r], local, *earlier],
+            [part_two, of((1 + len(earlier), *part_two.shape), BF16)],
             2 * one // OWNERS,
         )
-    received[last] = swap(send, pair)
-    early = 1
+        if not whole:
+            waiting.append(send)
+            continue
+        if k + 1 < OWNERS:
+            bases[ARRIVAL[k + 1]], send = lax.optimization_barrier((bases[ARRIVAL[k + 1]], send))
+        got = swap(send, pair)
+        for n in range(1 + len(earlier)):
+            received[ARRIVAL[k - len(earlier) + n]] = (got, n)
+        waiting = []
     attended, grad_queries, grad_keys, grad_values = call(
-        functools.partial(join_most_kernel, early),
-        [attended, grad_queries, swapped, *own, *(received[r] for r in ARRIVAL[:early])],
+        functools.partial(join_most_kernel, 0),
+        [attended, grad_queries, swapped, *own],
         [full] * 4,
         hbm_out=True,
-        scratch=[sems((1 + OWNERS + early, 2))],
+        scratch=[sems((1 + OWNERS, 2))],
         alias=2,
     )
+    sources = []
+    for got, _ in received:
+        if not any(got is source for source in sources):
+            sources.append(got)
+    where = [next((k, n) for k, source in enumerate(sources) if source is got) for got, n in received]
     grad_keys, grad_values = call(
-        functools.partial(join_rest_kernel, early),
-        [grad_keys, grad_values, *(received[r] for r in ARRIVAL[early:])],
+        functools.partial(join_rest_kernel, where),
+        [grad_keys, grad_values, *sources],
         [full] * 2,
         hbm_out=True,
-        scratch=[sems((OWNERS - early, 2))],
+        scratch=[sems((OWNERS, 2))],
         alias=2,
     )
     return (attended, grad_queries, grad_keys, grad_values)

time: 74.4 us -> 74.1 us (level)
    ppermute x27 -> x25, waiting for transfers between devices: 29.4 us -> 30 us  [swap(): return lax.ppermute(x, AXES, [(i, i ^ bits) for i in range(count)])]
    ppermute x27 -> x25, starting transfers between devices: 28.6 us -> 28 us  [swap(): return lax.ppermute(x, AXES, [(i, i ^ bits) for i in range(count)])]
  transfers between devices with their start and end apart: 27 -> 25, of which waited for: 12 -> 13; matrix products, arithmetic and copies ran while one was open for 0% -> 0% of each run, Pallas kernels for 16% -> 16%
where the time goes in v3:
time: 74.1 us; the launch traced here: 74 us
  waiting for transfers between devices  30 us (40%)
  starting transfers between devices  28 us (38%)
  Pallas kernels  14.8 us (20%)
  between operations  0.9 us (1%)
    ppermute x25, waiting for transfers between devices, swap(): return lax.ppermute(x, AXES, [(i, i ^ bits) for i in range(count)])  30 us
    ppermute x25, starting transfers between devices, swap(): return lax.ppermute(x, AXES, [(i, i ^ bits) for i in range(count)])  28 us
    pallas_call x26, Pallas kernels, call(): pl.pallas_call(kernel, out_shape=list(outs), in_specs=[pl.BlockSpec(memor...  14.8 us
  transfers between devices with their start and end apart: 25, of which 13 were waited for; matrix products, arithmetic and copies ran while one was open for 0% of the time, Pallas kernels for 16%

profile of v3, /device:TPU:0, one launch (start us, length us, event | category | flops | bytes accessed | tf_op | source)
XLA Modules:
  0.0 74.0 jit_solution(2077996843923879076)
XLA Ops:
  0.6 1.1 %shard_map.76 = bf16[2,128,1024]{2,1,0:T(8,128)(2,1)S(1)} custom-call(bf16[128,2048]{1,0:T(8,128)(2,1)} %a.3, bf16[128,2048]{1,0:T(8,128)(2,1)} %b.3), custom_call_target="tpu_custom_call" | custom-call | bytes 1572864 | tf_op jit(solution)/shard_map/pallas_call | solution.py:63
  1.7 0.6 collective-permute-start
  2.3 1.0 %shard_map.75.own.kv.kv_own = bf16[2,128,1024]{2,1,0:T(8,128)(2,1)S(1)} custom-call(bf16[128,2048]{1,0:T(8,128)(2,1)} %a.3, bf16[128,2048]{1,0:T(8,128)(2,1)} %b.3), custom_call_target="tpu_custom_call" | custom-call | bytes 1572864 | tf_op jit(solution)/shard_map/pallas_call | solution.py:63
  3.3 0.5 collective-permute-done.other.kv.kv_other
  3.8 0.5 shard_map.77
  4.8 2.8 %collective-permute-start.8 = (bf16[4,2,2,128,128]{4,3,2,1,0:T(8,128)(2,1)S(1)}, bf16[4,2,2,128,128]{4,3,2,1,0:T(8,128)(2,1)S(1)}, u32[]{:S(2)}, u32[]{:S(2)}) collective-permute-start(bf16[4,2,2,128,128]{4,3,2,1,0:T(8,128)(2,1)S(1)} %get-tuple-element.122.every), channel_id=1, source_target_pairs={{0,1},{1,0},{2,3},{3,2},{4,5},{5,4},{6,7},{7,6},{8,9},{9,8},{10,11... | collective-permute-start | bytes 1572872 | tf_op jit(solution)/shard_map/ppermute | solution.py:56
  7.7 2.0 %collective-permute-start.3 = (bf16[2,128,128]{2,1,0:T(8,128)(2,1)S(1)}, bf16[2,128,128]{2,1,0:T(8,128)(2,1)S(1)}, u32[]{:S(2)}, u32[]{:S(2)}) collective-permute-start(bf16[2,128,128]{2,1,0:T(8,128)(2,1)S(1)} %get-tuple-element.110), channel_id=1, source_target_pairs={{0,4},{1,5},{2,6},{3,7},{4,0},{5,1},{6,2},{7,3},{8,12},{9,13},{10,... | collective-permute-start | bytes 196616 | tf_op jit(solution)/shard_map/ppermute | solution.py:56
  9.7 1.4 %collective-permute-start.4 = (bf16[2,128,128]{2,1,0:T(8,128)(2,1)S(1)}, bf16[2,128,128]{2,1,0:T(8,128)(2,1)S(1)}, u32[]{:S(2)}, u32[]{:S(2)}) collective-permute-start(bf16[2,128,128]{2,1,0:T(8,128)(2,1)S(1)} %get-tuple-element.111), channel_id=1, source_target_pairs={{0,5},{1,4},{2,7},{3,6},{4,1},{5,0},{6,3},{7,2},{8,13},{9,12},{10,... | collective-permute-start | bytes 196616 | tf_op jit(solution)/shard_map/ppermute | solution.py:56
  11.1 10.7 %collective-permute-done.2.refs_1_ = bf16[2,128,128]{2,1,0:T(8,128)(2,1)S(1)} collective-permute-done((bf16[2,128,128]{2,1,0:T(8,128)(2,1)S(1)}, bf16[2,128,128]{2,1,0:T(8,128)(2,1)S(1)}, u32[]{:S(2)}, u32[]{:S(2)}) %collective-permute-start.2) | collective-permute-done | bytes 65568 | tf_op jit(solution)/shard_map/ppermute | solution.py:56
  21.8 2.1 %collective-permute-done.4.refs_3_ = bf16[2,128,128]{2,1,0:T(8,128)(2,1)S(1)} collective-permute-done((bf16[2,128,128]{2,1,0:T(8,128)(2,1)S(1)}, bf16[2,128,128]{2,1,0:T(8,128)(2,1)S(1)}, u32[]{:S(2)}, u32[]{:S(2)}) %collective-permute-start.4) | collective-permute-done | bytes 65568 | tf_op jit(solution)/shard_map/ppermute | solution.py:56
  23.9 1.6 %collective-permute-start.7 = (bf16[2,128,128]{2,1,0:T(8,128)(2,1)S(1)}, bf16[2,128,128]{2,1,0:T(8,128)(2,1)S(1)}, u32[]{:S(2)}, u32[]{:S(2)}) collective-permute-start(bf16[2,128,128]{2,1,0:T(8,128)(2,1)S(1)} %shard_map.80), channel_id=1, source_target_pairs={{0,8},{1,9},{2,10},{3,11},{4,12},{5,13},{6,14},{7,15},{8,0},{9,1},... | collective-permute-start | bytes 196616 | tf_op jit(solution)/shard_map/ppermute | solution.py:56
  25.6 2.6 %collective-permute-start.6 = (bf16[2,128,128]{2,1,0:T(8,128)(2,1)S(1)}, bf16[2,128,128]{2,1,0:T(8,128)(2,1)S(1)}, u32[]{:S(2)}, u32[]{:S(2)}) collective-permute-start(bf16[2,128,128]{2,1,0:T(8,128)(2,1)S(1)} %shard_map.80), channel_id=1, source_target_pairs={{0,16},{1,17},{2,18},{3,19},{4,20},{5,21},{6,22},{7,23},{8,24},{9,... | collective-permute-start | bytes 196616 | tf_op jit(solution)/shard_map/ppermute | solution.py:56
  28.5 1.3 %shard_map.81 = (bf16[8,128,128]{2,1,0:T(8,128)(2,1)S(1)}, f32[128,1024]{1,0:T(8,128)S(1)}) custom-call(bf16[2,128,1024]{2,1,0:T(8,128)(2,1)S(1)} %shard_map.78.qg.qg_own, bf16[2,128,1024]{2,1,0:T(8,128)(2,1)S(1)} %shard_map.75.own.kv.kv_own), custom_call_target="tpu_custom_call" | custom-call | flops 67108864 | bytes 1835008 | tf_op jit(solution)/shard_map/pallas_call | solution.py:63
  29.8 1.3 %shard_map.82 = (bf16[8,128,128]{2,1,0:T(8,128)(2,1)S(1)}, f32[128,1024]{1,0:T(8,128)S(1)}) custom-call(bf16[2,128,1024]{2,1,0:T(8,128)(2,1)S(1)} %collective-permute-done.1.qg.qg_other, bf16[2,128,1024]{2,1,0:T(8,128)(2,1)S(1)} %collective-permute-done.other.kv.kv_other), custom_call_target="tpu_custom_call" | custom-call | flops 67108864 | bytes 1835008 | tf_op jit(solution)/shard_map/pallas_call | solution.py:63
  31.2 1.0 %collective-permute-done.6.refs_5_ = bf16[2,128,128]{2,1,0:T(8,128)(2,1)S(1)} collective-permute-done((bf16[2,128,128]{2,1,0:T(8,128)(2,1)S(1)}, bf16[2,128,128]{2,1,0:T(8,128)(2,1)S(1)}, u32[]{:S(2)}, u32[]{:S(2)}) %collective-permute-start.6) | collective-permute-done | bytes 65568 | tf_op jit(solution)/shard_map/ppermute | solution.py:56
  32.2 2.1 %collective-permute-done.5.refs_4_ = bf16[2,128,128]{2,1,0:T(8,128)(2,1)S(1)} collective-permute-done((bf16[2,128,128]{2,1,0:T(8,128)(2,1)S(1)}, bf16[2,128,128]{2,1,0:T(8,128)(2,1)S(1)}, u32[]{:S(2)}, u32[]{:S(2)}) %collective-permute-start.5) | collective-permute-done | bytes 65568 | tf_op jit(solution)/shard_map/ppermute | solution.py:56
  34.3 0.6 collective-permute-start.10
  34.9 2.4 %collective-permute-start.11 = (bf16[2,128,128]{2,1,0:T(8,128)(2,1)S(1)}, bf16[2,128,128]{2,1,0:T(8,128)(2,1)S(1)}, u32[]{:S(2)}, u32[]{:S(2)}) collective-permute-start(bf16[2,128,128]{2,1,0:T(8,128)(2,1)S(1)} %get-tuple-element.125), channel_id=1, source_target_pairs={{0,5},{1,4},{2,7},{3,6},{4,1},{5,0},{6,3},{7,2},{8,13},{9,12},{10,... | collective-permute-start | bytes 196616 | tf_op jit(solution)/shard_map/ppermute | solution.py:56
  37.3 0.5 collective-permute-start.9
  37.9 0.3 shard_map.84.local
  38.2 0.5 shard_map.85
  38.7 0.5 shard_map.87
  39.2 0.8 %collective-permute-done.11.base = bf16[2,128,128]{2,1,0:T(8,128)(2,1)S(1)} collective-permute-done((bf16[2,128,128]{2,1,0:T(8,128)(2,1)S(1)}, bf16[2,128,128]{2,1,0:T(8,128)(2,1)S(1)}, u32[]{:S(2)}, u32[]{:S(2)}) %collective-permute-start.11) | collective-permute-done | bytes 65568 | tf_op jit(solution)/shard_map/ppermute | solution.py:56
  40.1 0.5 shard_map.88
  40.6 1.7 %collective-permute-done.9.base = bf16[2,128,128]{2,1,0:T(8,128)(2,1)S(1)} collective-permute-done((bf16[2,128,128]{2,1,0:T(8,128)(2,1)S(1)}, bf16[2,128,128]{2,1,0:T(8,128)(2,1)S(1)}, u32[]{:S(2)}, u32[]{:S(2)}) %collective-permute-start.9) | collective-permute-done | bytes 65568 | tf_op jit(solution)/shard_map/ppermute | solution.py:56
  42.3 0.5 shard_map.86
  42.9 0.9 %collective-permute-start.19 = (bf16[4,2,2,128,128]{4,3,2,1,0:T(8,128)(2,1)S(1)}, bf16[4,2,2,128,128]{4,3,2,1,0:T(8,128)(2,1)S(1)}, u32[]{:S(2)}, u32[]{:S(2)}) collective-permute-start(bf16[4,2,2,128,128]{4,3,2,1,0:T(8,128)(2,1)S(1)} %shard_map.93.every), channel_id=1, source_target_pairs={{0,1},{1,0},{2,3},{3,2},{4,5},{5,4},{6,7},{7,6},{8,9},{9,8},{10,11... | collective-permute-start | bytes 1572872 | tf_op jit(solution)/shard_map/ppermute | solution.py:56
  43.8 0.6 collective-permute-start.13
  44.4 2.1 %collective-permute-start.14 = (bf16[2,128,128]{2,1,0:T(8,128)(2,1)S(1)}, bf16[2,128,128]{2,1,0:T(8,128)(2,1)S(1)}, u32[]{:S(2)}, u32[]{:S(2)}) collective-permute-start(bf16[2,128,128]{2,1,0:T(8,128)(2,1)S(1)} %get-tuple-element.131), channel_id=1, source_target_pairs={{0,5},{1,4},{2,7},{3,6},{4,1},{5,0},{6,3},{7,2},{8,13},{9,12},{10,... | collective-permute-start | bytes 196616 | tf_op jit(solution)/shard_map/ppermute | solution.py:56
  46.5 0.8 %collective-permute-start.12 = (bf16[2,128,128]{2,1,0:T(8,128)(2,1)S(1)}, bf16[2,128,128]{2,1,0:T(8,128)(2,1)S(1)}, u32[]{:S(2)}, u32[]{:S(2)}) collective-permute-start(bf16[2,128,128]{2,1,0:T(8,128)(2,1)S(1)} %get-tuple-element.129), channel_id=1, source_target_pairs={{0,1},{1,0},{2,3},{3,2},{4,5},{5,4},{6,7},{7,6},{8,9},{9,8},{10,11... | collective-permute-start | bytes 196616 | tf_op jit(solution)/shard_map/ppermute | solution.py:56
  47.3 1.1 %collective-permute-done.13.refs_2_ = bf16[2,128,128]{2,1,0:T(8,128)(2,1)S(1)} collective-permute-done((bf16[2,128,128]{2,1,0:T(8,128)(2,1)S(1)}, bf16[2,128,128]{2,1,0:T(8,128)(2,1)S(1)}, u32[]{:S(2)}, u32[]{:S(2)}) %collective-permute-start.13) | collective-permute-done | bytes 65568 | tf_op jit(solution)/shard_map/ppermute | solution.py:56
  48.4 6.5 %collective-permute-done.14.refs_3_ = bf16[2,128,128]{2,1,0:T(8,128)(2,1)S(1)} collective-permute-done((bf16[2,128,128]{2,1,0:T(8,128)(2,1)S(1)}, bf16[2,128,128]{2,1,0:T(8,128)(2,1)S(1)}, u32[]{:S(2)}, u32[]{:S(2)}) %collective-permute-start.14) | collective-permute-done | bytes 65568 | tf_op jit(solution)/shard_map/ppermute | solution.py:56
  54.8 0.5 collective-permute-done.12.refs_1_
  55.4 1.9 %collective-permute-start.16 = (bf16[2,128,128]{2,1,0:T(8,128)(2,1)S(1)}, bf16[2,128,128]{2,1,0:T(8,128)(2,1)S(1)}, u32[]{:S(2)}, u32[]{:S(2)}) collective-permute-start(bf16[2,128,128]{2,1,0:T(8,128)(2,1)S(1)} %shard_map.89), channel_id=1, source_target_pairs={{0,16},{1,17},{2,18},{3,19},{4,20},{5,21},{6,22},{7,23},{8,24},{9,... | collective-permute-start | bytes 196616 | tf_op jit(solution)/shard_map/ppermute | solution.py:56
  57.3 2.5 %collective-permute-start.15 = (bf16[2,128,128]{2,1,0:T(8,128)(2,1)S(1)}, bf16[2,128,128]{2,1,0:T(8,128)(2,1)S(1)}, u32[]{:S(2)}, u32[]{:S(2)}) collective-permute-start(bf16[2,128,128]{2,1,0:T(8,128)(2,1)S(1)} %shard_map.89), channel_id=1, source_target_pairs={{0,24},{1,25},{2,26},{3,27},{4,28},{5,29},{6,30},{7,31},{8,16},{9,... | collective-permute-start | bytes 196616 | tf_op jit(solution)/shard_map/ppermute | solution.py:56
  59.8 2.7 %shard_map.90 = (bf16[128,1024]{1,0:T(8,128)(2,1)S(1)}, bf16[2,128,1024]{2,1,0:T(8,128)(2,1)S(1)}, f32[2,128,1024]{2,1,0:T(8,128)S(1)}, f32[2,128,1024]{2,1,0:T(8,128)S(1)}) custom-call(bf16[2,128,1024]{2,1,0:T(8,128)(2,1)S(1)} %shard_map.78.qg.qg_own, bf16[2,128,1024]{2,1,0:T(8,128)(2,1)S(1)} %collective-permute-done.1.qg.qg_other, ...), custom_call_target="tpu_custom_call" | custom-call | flops 335544320 | bytes 6815744 | tf_op jit(solution)/shard_map/pallas_call | solution.py:63
  62.5 0.9 %collective-permute-done.15.refs_4_ = bf16[2,128,128]{2,1,0:T(8,128)(2,1)S(1)} collective-permute-done((bf16[2,128,128]{2,1,0:T(8,128)(2,1)S(1)}, bf16[2,128,128]{2,1,0:T(8,128)(2,1)S(1)}, u32[]{:S(2)}, u32[]{:S(2)}) %collective-permute-start.15) | collective-permute-done | bytes 65568 | tf_op jit(solution)/shard_map/ppermute | solution.py:56
  63.5 1.1 %collective-permute-start.21 = (bf16[2,128,128]{2,1,0:T(8,128)(2,1)S(1)}, bf16[2,128,128]{2,1,0:T(8,128)(2,1)S(1)}, u32[]{:S(2)}, u32[]{:S(2)}) collective-permute-start(bf16[2,128,128]{2,1,0:T(8,128)(2,1)S(1)} %get-tuple-element.185), channel_id=1, source_target_pairs={{0,5},{1,4},{2,7},{3,6},{4,1},{5,0},{6,3},{7,2},{8,13},{9,12},{10,... | collective-permute-start | bytes 196616 | tf_op jit(solution)/shard_map/ppermute | solution.py:56
  64.6 1.2 %collective-permute-start.20 = (bf16[2,128,128]{2,1,0:T(8,128)(2,1)S(1)}, bf16[2,128,128]{2,1,0:T(8,128)(2,1)S(1)}, u32[]{:S(2)}, u32[]{:S(2)}) collective-permute-start(bf16[2,128,128]{2,1,0:T(8,128)(2,1)S(1)} %get-tuple-element.178.base), channel_id=1, source_target_pairs={{0,1},{1,0},{2,3},{3,2},{4,5},{5,4},{6,7},{7,6},{8,9},{9,8},{10,11... | collective-permute-start | bytes 196616 | tf_op jit(solution)/shard_map/ppermute | solution.py:56
  65.8 1.3 %collective-permute-start.22 = (bf16[2,128,128]{2,1,0:T(8,128)(2,1)S(1)}, bf16[2,128,128]{2,1,0:T(8,128)(2,1)S(1)}, u32[]{:S(2)}, u32[]{:S(2)}) collective-permute-start(bf16[2,128,128]{2,1,0:T(8,128)(2,1)S(1)} %get-tuple-element.185), channel_id=1, source_target_pairs={{0,4},{1,5},{2,6},{3,7},{4,0},{5,1},{6,2},{7,3},{8,12},{9,13},{10,... | collective-permute-start | bytes 196616 | tf_op jit(solution)/shard_map/ppermute | solution.py:56
  67.0 0.3 shard_map.94.local
  67.5 1.8 %collective-permute-done.21.base = bf16[2,128,128]{2,1,0:T(8,128)(2,1)S(1)} collective-permute-done((bf16[2,128,128]{2,1,0:T(8,128)(2,1)S(1)}, bf16[2,128,128]{2,1,0:T(8,128)(2,1)S(1)}, u32[]{:S(2)}, u32[]{:S(2)}) %collective-permute-start.21) | collective-permute-done | bytes 65568 | tf_op jit(solution)/shard_map/ppermute | solution.py:56
  69.7 0.3 shard_map.97
  69.9 0.4 collective-permute-done.22.base
  70.6 0.6 collective-permute-start.24
  71.2 0.8 %shard_map.91 = (bf16[128,2048]{1,0:T(8,128)(2,1)}, bf16[128,2048]{1,0:T(8,128)(2,1)}) custom-call(bf16[128,256]{1,0:T(8,128)(2,1)S(1)} %get-tuple-element.123.refs_0_, bf16[128,256]{1,0:T(8,128)(2,1)S(1)} %get-tuple-element.124.refs_1_, bf16[128,256]{1,0:T(8,128)(2,1)S(1)} %get-tuple-element.126.refs_2_, bf16[128,256]{1,0:T(8,128)(2,1)S(1)} %get-tuple-element.127.refs_3_, ...), custom_call_target="tpu_custom_call" | custom-call | bytes 1572864 | tf_op jit(solution)/shard_map/pallas_call | solution.py:63
  72.0 1.1 %shard_map.99 = (bf16[128,2048]{1,0:T(8,128)(2,1)}, bf16[128,2048]{1,0:T(8,128)(2,1)}, bf16[128,2048]{1,0:T(8,128)(2,1)}, bf16[128,2048]{1,0:T(8,128)(2,1)}) custom-call(bf16[128,2048]{1,0:T(8,128)(2,1)} %get-tuple-element.170.refs_0_, bf16[128,2048]{1,0:T(8,128)(2,1)} %get-tuple-element.171.refs_1_, ...), custom_call_target="tpu_custom_call", output_to_operand_aliasing={{0}: (0, {}), {1}: (1, {})} | custom-call | bytes 4194304 | tf_op jit(solution)/shard_map/pallas_call | solution.py:63
  73.1 0.9 %shard_map.100 = (bf16[128,2048]{1,0:T(8,128)(2,1)}, bf16[128,2048]{1,0:T(8,128)(2,1)}) custom-call(bf16[128,2048]{1,0:T(8,128)(2,1)} %get-tuple-element.194.refs_0_, bf16[128,2048]{1,0:T(8,128)(2,1)} %get-tuple-element.195.refs_1_, bf16[3,2,128,256]{3,2,1,0:T(8,128)(2,1)S(1)} %collective-permute-done.23.refs_2_, ...), custom_call_target="tpu_custom_call", output_to_operand_aliasing={{0}: (0, {}), {1}: (1, {})} | custom-call | bytes 2621440 | tf_op jit(solution)/shard_map/pallas_call | solution.py:63
  (32 shorter events, 2.0 us)
Async XLA Ops:
  1.7 2.1 %collective-permute-start = (bf16[2,128,1024]{2,1,0:T(8,128)(2,1)S(1)}, bf16[2,128,1024]{2,1,0:T(8,128)(2,1)S(1)}, u32[]{:S(2)}, u32[]{:S(2)}) collective-permute-start(bf16[2,128,1024]{2,1,0:T(8,128)(2,1)S(1)} %shard_map.76), channel_id=1, source_target_pairs={{0,2},{1,3},{2,0},{3,1},{4,6},{5,7},{6,4},{7,5},{8,10},{9,11},{10,... | collective-permute-start | bytes 1572872 | tf_op jit(solution)/shard_map/ppermute | solution.py:56
  3.3 1.0 %copy-start = (bf16[128,2048]{1,0:T(8,128)(2,1)S(1)}, bf16[128,2048]{1,0:T(8,128)(2,1)}, u32[]{:S(2)}) copy-start(bf16[128,2048]{1,0:T(8,128)(2,1)} %a.5) | copy-start | bytes 1572868
  3.3 1.2 %copy-start.1 = (bf16[128,2048]{1,0:T(8,128)(2,1)S(1)}, bf16[128,2048]{1,0:T(8,128)(2,1)}, u32[]{:S(2)}) copy-start(bf16[128,2048]{1,0:T(8,128)(2,1)} %b.5) | copy-start | bytes 1572868
  4.6 25.2 %collective-permute-start.1 = (bf16[2,128,1024]{2,1,0:T(8,128)(2,1)S(1)}, bf16[2,128,1024]{2,1,0:T(8,128)(2,1)S(1)}, u32[]{:S(2)}, u32[]{:S(2)}) collective-permute-start(bf16[2,128,1024]{2,1,0:T(8,128)(2,1)S(1)} %shard_map.79), channel_id=1, source_target_pairs={{0,2},{1,3},{2,0},{3,1},{4,6},{5,7},{6,4},{7,5},{8,10},{9,11},{10,... | collective-permute-start | bytes 1572872 | tf_op jit(solution)/shard_map/ppermute | solution.py:56
  4.8 33.1 %collective-permute-start.8 = (bf16[4,2,2,128,128]{4,3,2,1,0:T(8,128)(2,1)S(1)}, bf16[4,2,2,128,128]{4,3,2,1,0:T(8,128)(2,1)S(1)}, u32[]{:S(2)}, u32[]{:S(2)}) collective-permute-start(bf16[4,2,2,128,128]{4,3,2,1,0:T(8,128)(2,1)S(1)} %get-tuple-element.122.every), channel_id=1, source_target_pairs={{0,1},{1,0},{2,3},{3,2},{4,5},{5,4},{6,7},{7,6},{8,9},{9,8},{10,11... | collective-permute-start | bytes 1572872 | tf_op jit(solution)/shard_map/ppermute | solution.py:56
  7.6 14.2 %collective-permute-start.2 = (bf16[2,128,128]{2,1,0:T(8,128)(2,1)S(1)}, bf16[2,128,128]{2,1,0:T(8,128)(2,1)S(1)}, u32[]{:S(2)}, u32[]{:S(2)}) collective-permute-start(bf16[2,128,128]{2,1,0:T(8,128)(2,1)S(1)} %get-tuple-element.109), channel_id=1, source_target_pairs={{0,1},{1,0},{2,3},{3,2},{4,5},{5,4},{6,7},{7,6},{8,9},{9,8},{10,11... | collective-permute-start | bytes 196616 | tf_op jit(solution)/shard_map/ppermute | solution.py:56
  7.7 14.2 %collective-permute-start.3 = (bf16[2,128,128]{2,1,0:T(8,128)(2,1)S(1)}, bf16[2,128,128]{2,1,0:T(8,128)(2,1)S(1)}, u32[]{:S(2)}, u32[]{:S(2)}) collective-permute-start(bf16[2,128,128]{2,1,0:T(8,128)(2,1)S(1)} %get-tuple-element.110), channel_id=1, source_target_pairs={{0,4},{1,5},{2,6},{3,7},{4,0},{5,1},{6,2},{7,3},{8,12},{9,13},{10,... | collective-permute-start | bytes 196616 | tf_op jit(solution)/shard_map/ppermute | solution.py:56
  9.7 14.2 %collective-permute-start.4 = (bf16[2,128,128]{2,1,0:T(8,128)(2,1)S(1)}, bf16[2,128,128]{2,1,0:T(8,128)(2,1)S(1)}, u32[]{:S(2)}, u32[]{:S(2)}) collective-permute-start(bf16[2,128,128]{2,1,0:T(8,128)(2,1)S(1)} %get-tuple-element.111), channel_id=1, source_target_pairs={{0,5},{1,4},{2,7},{3,6},{4,1},{5,0},{6,3},{7,2},{8,13},{9,12},{10,... | collective-permute-start | bytes 196616 | tf_op jit(solution)/shard_map/ppermute | solution.py:56
  23.9 7.2 %collective-permute-start.7 = (bf16[2,128,128]{2,1,0:T(8,128)(2,1)S(1)}, bf16[2,128,128]{2,1,0:T(8,128)(2,1)S(1)}, u32[]{:S(2)}, u32[]{:S(2)}) collective-permute-start(bf16[2,128,128]{2,1,0:T(8,128)(2,1)S(1)} %shard_map.80), channel_id=1, source_target_pairs={{0,8},{1,9},{2,10},{3,11},{4,12},{5,13},{6,14},{7,15},{8,0},{9,1},... | collective-permute-start | bytes 196616 | tf_op jit(solution)/shard_map/ppermute | solution.py:56
  25.6 6.6 %collective-permute-start.6 = (bf16[2,128,128]{2,1,0:T(8,128)(2,1)S(1)}, bf16[2,128,128]{2,1,0:T(8,128)(2,1)S(1)}, u32[]{:S(2)}, u32[]{:S(2)}) collective-permute-start(bf16[2,128,128]{2,1,0:T(8,128)(2,1)S(1)} %shard_map.80), channel_id=1, source_target_pairs={{0,16},{1,17},{2,18},{3,19},{4,20},{5,21},{6,22},{7,23},{8,24},{9,... | collective-permute-start | bytes 196616 | tf_op jit(solution)/shard_map/ppermute | solution.py:56
  28.2 6.1 %collective-permute-start.5 = (bf16[2,128,128]{2,1,0:T(8,128)(2,1)S(1)}, bf16[2,128,128]{2,1,0:T(8,128)(2,1)S(1)}, u32[]{:S(2)}, u32[]{:S(2)}) collective-permute-start(bf16[2,128,128]{2,1,0:T(8,128)(2,1)S(1)} %shard_map.80), channel_id=1, source_target_pairs={{0,24},{1,25},{2,26},{3,27},{4,28},{5,29},{6,30},{7,31},{8,16},{9,... | collective-permute-start | bytes 196616 | tf_op jit(solution)/shard_map/ppermute | solution.py:56
  34.3 4.4 %collective-permute-start.10 = (bf16[2,128,128]{2,1,0:T(8,128)(2,1)S(1)}, bf16[2,128,128]{2,1,0:T(8,128)(2,1)S(1)}, u32[]{:S(2)}, u32[]{:S(2)}) collective-permute-start(bf16[2,128,128]{2,1,0:T(8,128)(2,1)S(1)} %get-tuple-element.125), channel_id=1, source_target_pairs={{0,4},{1,5},{2,6},{3,7},{4,0},{5,1},{6,2},{7,3},{8,12},{9,13},{10,... | collective-permute-start | bytes 196616 | tf_op jit(solution)/shard_map/ppermute | solution.py:56
  34.9 5.2 %collective-permute-start.11 = (bf16[2,128,128]{2,1,0:T(8,128)(2,1)S(1)}, bf16[2,128,128]{2,1,0:T(8,128)(2,1)S(1)}, u32[]{:S(2)}, u32[]{:S(2)}) collective-permute-start(bf16[2,128,128]{2,1,0:T(8,128)(2,1)S(1)} %get-tuple-element.125), channel_id=1, source_target_pairs={{0,5},{1,4},{2,7},{3,6},{4,1},{5,0},{6,3},{7,2},{8,13},{9,12},{10,... | collective-permute-start | bytes 196616 | tf_op jit(solution)/shard_map/ppermute | solution.py:56
  37.3 5.0 %collective-permute-start.9 = (bf16[2,128,128]{2,1,0:T(8,128)(2,1)S(1)}, bf16[2,128,128]{2,1,0:T(8,128)(2,1)S(1)}, u32[]{:S(2)}, u32[]{:S(2)}) collective-permute-start(bf16[2,128,128]{2,1,0:T(8,128)(2,1)S(1)} %get-tuple-element.121.base), channel_id=1, source_target_pairs={{0,1},{1,0},{2,3},{3,2},{4,5},{5,4},{6,7},{7,6},{8,9},{9,8},{10,11... | collective-permute-start | bytes 196616 | tf_op jit(solution)/shard_map/ppermute | solution.py:56
  42.9 24.1 %collective-permute-start.19 = (bf16[4,2,2,128,128]{4,3,2,1,0:T(8,128)(2,1)S(1)}, bf16[4,2,2,128,128]{4,3,2,1,0:T(8,128)(2,1)S(1)}, u32[]{:S(2)}, u32[]{:S(2)}) collective-permute-start(bf16[4,2,2,128,128]{4,3,2,1,0:T(8,128)(2,1)S(1)} %shard_map.93.every), channel_id=1, source_target_pairs={{0,1},{1,0},{2,3},{3,2},{4,5},{5,4},{6,7},{7,6},{8,9},{9,8},{10,11... | collective-permute-start | bytes 1572872 | tf_op jit(solution)/shard_map/ppermute | solution.py:56
  43.8 4.6 %collective-permute-start.13 = (bf16[2,128,128]{2,1,0:T(8,128)(2,1)S(1)}, bf16[2,128,128]{2,1,0:T(8,128)(2,1)S(1)}, u32[]{:S(2)}, u32[]{:S(2)}) collective-permute-start(bf16[2,128,128]{2,1,0:T(8,128)(2,1)S(1)} %get-tuple-element.130), channel_id=1, source_target_pairs={{0,4},{1,5},{2,6},{3,7},{4,0},{5,1},{6,2},{7,3},{8,12},{9,13},{10,... | collective-permute-start | bytes 196616 | tf_op jit(solution)/shard_map/ppermute | solution.py:56
  44.4 10.4 %collective-permute-start.14 = (bf16[2,128,128]{2,1,0:T(8,128)(2,1)S(1)}, bf16[2,128,128]{2,1,0:T(8,128)(2,1)S(1)}, u32[]{:S(2)}, u32[]{:S(2)}) collective-permute-start(bf16[2,128,128]{2,1,0:T(8,128)(2,1)S(1)} %get-tuple-element.131), channel_id=1, source_target_pairs={{0,5},{1,4},{2,7},{3,6},{4,1},{5,0},{6,3},{7,2},{8,13},{9,12},{10,... | collective-permute-start | bytes 196616 | tf_op jit(solution)/shard_map/ppermute | solution.py:56
  46.5 8.8 %collective-permute-start.12 = (bf16[2,128,128]{2,1,0:T(8,128)(2,1)S(1)}, bf16[2,128,128]{2,1,0:T(8,128)(2,1)S(1)}, u32[]{:S(2)}, u32[]{:S(2)}) collective-permute-start(bf16[2,128,128]{2,1,0:T(8,128)(2,1)S(1)} %get-tuple-element.129), channel_id=1, source_target_pairs={{0,1},{1,0},{2,3},{3,2},{4,5},{5,4},{6,7},{7,6},{8,9},{9,8},{10,11... | collective-permute-start | bytes 196616 | tf_op jit(solution)/shard_map/ppermute | solution.py:56
  55.3 7.1 %collective-permute-start.17 = (bf16[2,128,128]{2,1,0:T(8,128)(2,1)S(1)}, bf16[2,128,128]{2,1,0:T(8,128)(2,1)S(1)}, u32[]{:S(2)}, u32[]{:S(2)}) collective-permute-start(bf16[2,128,128]{2,1,0:T(8,128)(2,1)S(1)} %shard_map.89), channel_id=1, source_target_pairs={{0,8},{1,9},{2,10},{3,11},{4,12},{5,13},{6,14},{7,15},{8,0},{9,1},... | collective-permute-start | bytes 196616 | tf_op jit(solution)/shard_map/ppermute | solution.py:56
  55.4 7.1 %collective-permute-start.16 = (bf16[2,128,128]{2,1,0:T(8,128)(2,1)S(1)}, bf16[2,128,128]{2,1,0:T(8,128)(2,1)S(1)}, u32[]{:S(2)}, u32[]{:S(2)}) collective-permute-start(bf16[2,128,128]{2,1,0:T(8,128)(2,1)S(1)} %shard_map.89), channel_id=1, source_target_pairs={{0,16},{1,17},{2,18},{3,19},{4,20},{5,21},{6,22},{7,23},{8,24},{9,... | collective-permute-start | bytes 196616 | tf_op jit(solution)/shard_map/ppermute | solution.py:56
  57.3 6.1 %collective-permute-start.15 = (bf16[2,128,128]{2,1,0:T(8,128)(2,1)S(1)}, bf16[2,128,128]{2,1,0:T(8,128)(2,1)S(1)}, u32[]{:S(2)}, u32[]{:S(2)}) collective-permute-start(bf16[2,128,128]{2,1,0:T(8,128)(2,1)S(1)} %shard_map.89), channel_id=1, source_target_pairs={{0,24},{1,25},{2,26},{3,27},{4,28},{5,29},{6,30},{7,31},{8,16},{9,... | collective-permute-start | bytes 196616 | tf_op jit(solution)/shard_map/ppermute | solution.py:56
  63.4 8.6 %collective-permute-start.18 = (bf16[2,128,1024]{2,1,0:T(8,128)(2,1)S(1)}, bf16[2,128,1024]{2,1,0:T(8,128)(2,1)S(1)}, u32[]{:S(2)}, u32[]{:S(2)}) collective-permute-start(bf16[2,128,1024]{2,1,0:T(8,128)(2,1)S(1)} %get-tuple-element.172), channel_id=1, source_target_pairs={{0,2},{1,3},{2,0},{3,1},{4,6},{5,7},{6,4},{7,5},{8,10},{9,11},{10,... | collective-permute-start | bytes 1572872 | tf_op jit(solution)/shard_map/ppermute | solution.py:56
  63.5 5.9 %collective-permute-start.21 = (bf16[2,128,128]{2,1,0:T(8,128)(2,1)S(1)}, bf16[2,128,128]{2,1,0:T(8,128)(2,1)S(1)}, u32[]{:S(2)}, u32[]{:S(2)}) collective-permute-start(bf16[2,128,128]{2,1,0:T(8,128)(2,1)S(1)} %get-tuple-element.185), channel_id=1, source_target_pairs={{0,5},{1,4},{2,7},{3,6},{4,1},{5,0},{6,3},{7,2},{8,13},{9,12},{10,... | collective-permute-start | bytes 196616 | tf_op jit(solution)/shard_map/ppermute | solution.py:56
  64.6 5.1 %collective-permute-start.20 = (bf16[2,128,128]{2,1,0:T(8,128)(2,1)S(1)}, bf16[2,128,128]{2,1,0:T(8,128)(2,1)S(1)}, u32[]{:S(2)}, u32[]{:S(2)}) collective-permute-start(bf16[2,128,128]{2,1,0:T(8,128)(2,1)S(1)} %get-tuple-element.178.base), channel_id=1, source_target_pairs={{0,1},{1,0},{2,3},{3,2},{4,5},{5,4},{6,7},{7,6},{8,9},{9,8},{10,11... | collective-permute-start | bytes 196616 | tf_op jit(solution)/shard_map/ppermute | solution.py:56
  65.8 4.6 %collective-permute-start.22 = (bf16[2,128,128]{2,1,0:T(8,128)(2,1)S(1)}, bf16[2,128,128]{2,1,0:T(8,128)(2,1)S(1)}, u32[]{:S(2)}, u32[]{:S(2)}) collective-permute-start(bf16[2,128,128]{2,1,0:T(8,128)(2,1)S(1)} %get-tuple-element.185), channel_id=1, source_target_pairs={{0,4},{1,5},{2,6},{3,7},{4,0},{5,1},{6,2},{7,3},{8,12},{9,13},{10,... | collective-permute-start | bytes 196616 | tf_op jit(solution)/shard_map/ppermute | solution.py:56
  70.3 2.8 %collective-permute-start.23 = (bf16[3,2,128,256]{3,2,1,0:T(8,128)(2,1)S(1)}, bf16[3,2,128,256]{3,2,1,0:T(8,128)(2,1)S(1)}, u32[]{:S(2)}, u32[]{:S(2)}) collective-permute-start(bf16[3,2,128,256]{3,2,1,0:T(8,128)(2,1)S(1)} %get-tuple-element.196), channel_id=1, source_target_pairs={{0,2},{1,3},{2,0},{3,1},{4,6},{5,7},{6,4},{7,5},{8,10},{9,11},{10,... | collective-permute-start | bytes 1179656 | tf_op jit(solution)/shard_map/ppermute | solution.py:56
  70.6 2.5 %collective-permute-start.24 = (bf16[1,2,128,256]{3,2,1,0:T(8,128)(2,1)S(1)}, bf16[1,2,128,256]{3,2,1,0:T(8,128)(2,1)S(1)}, u32[]{:S(2)}, u32[]{:S(2)}) collective-permute-start(bf16[1,2,128,256]{3,2,1,0:T(8,128)(2,1)S(1)} %get-tuple-element.197), channel_id=1, source_target_pairs={{0,2},{1,3},{2,0},{3,1},{4,6},{5,7},{6,4},{7,5},{8,10},{9,11},{10,... | collective-permute-start | bytes 393224 | tf_op jit(solution)/shard_map/ppermute | solution.py:56
